TPU v7x, 32 devices: a whole 2x2x4 slice. The times are simulated.
32 devices in a mesh: dp: 8 (over z, y), tensor: 4 (over x, core).
Axes of the slice: x: 2, y: 2, z: 4, core: 2. Of those that a mesh axis runs over, the one named last changes fastest.
Arguments:
- block_input: bfloat16 [25088, 768], P(('dp', 'tensor')), may hold values from -6 to 6
- cotangent: bfloat16 [25088, 768], P(('dp', 'tensor')), may hold values from -6 to 6
- pad_mask: int32 [128, 196], replicated, may hold values from 0 to 1, as said below
- slot_window: int32 [128], P('dp'), may hold values from -1 to 127, as said below
- qkv_w: bfloat16 [3, 768, 768], P(None, 'dp', 'tensor'), may hold values from -0.21875 to 0.21875
- proj_w: bfloat16 [768, 768], P('tensor', 'dp'), may hold values from -1.25 to 1.25
- fc1_w: bfloat16 [768, 3072], P('dp', 'tensor'), may hold values from -0.21875 to 0.21875
- fc2_w: bfloat16 [3072, 768], P('tensor', 'dp'), may hold values from -0.109375 to 0.109375
- norm1_gain: float32 [768], replicated, may hold values from 0.5 to 1.5
- norm1_bias: float32 [768], replicated, may hold values from -3 to 3
- q_bias: float32 [768], replicated, may hold values from -3 to 3
- v_bias: float32 [768], replicated, may hold values from -3 to 3
- rel_h: float32 [27, 64], replicated, may hold values from -0.9 to 0.9
- rel_w: float32 [27, 64], replicated, may hold values from -0.9 to 0.9
- proj_bias: float32 [768], replicated, may hold values from -3 to 3
- norm2_gain: float32 [768], replicated, may hold values from 0.5 to 1.5
- norm2_bias: float32 [768], replicated, may hold values from -3 to 3
- fc1_bias: float32 [3072], replicated, may hold values from -3 to 3
- fc2_bias: float32 [768], replicated, may hold values from -3 to 3
Outputs:
- result: bfloat16 [25088, 768], P(('dp', 'tensor'))
- grad_x: bfloat16 [25088, 768], P(('dp', 'tensor'))
- grad_qkv_w: float32 [3, 768, 768], P(None, 'dp', 'tensor')
- grad_proj_w: float32 [768, 768], P('tensor', 'dp')
- grad_fc1_w: float32 [768, 3072], P('dp', 'tensor')
- grad_fc2_w: float32 [3072, 768], P('tensor', 'dp')
- grad_norm1_gain: float32 [768], replicated
- grad_norm1_bias: float32 [768], replicated
- grad_q_bias: float32 [768], replicated
- grad_v_bias: float32 [768], replicated
- grad_rel_h: float32 [27, 64], replicated
- grad_rel_w: float32 [27, 64], replicated
- grad_proj_bias: float32 [768], replicated
- grad_norm2_gain: float32 [768], replicated
- grad_norm2_bias: float32 [768], replicated
- grad_fc1_bias: float32 [3072], replicated
- grad_fc2_bias: float32 [768], replicated
Inputs may be any that keep to these rules, and one draw needn't show every extreme that they name: In each window the tokens with pad_mask 1 form a rectangle of 4 to 14 rows by 4 to 14 columns at the window's first row and column. `slot_window`: on each index of dp the first slots hold windows and the rest are empty (-1); each index of dp holds 8 to 16 windows, and some index holds 16; no window is named twice.
All inputs are finite; a program needn't handle non-finite values.
Results may differ from a plain program's by a relative error of at most 0.019.
Values may be sent and summed in bfloat16 or wider, within the bound.
A program may use at most 192 MiB of HBM per device.

v0:
```python
from functools import partial

import jax
import jax.numpy as jnp
from jax import lax
from jax.sharding import PartitionSpec as P

HD = 64


EPSILON = 1e-06
NEGATIVE = -1e30
HIGH = lax.Precision.HIGHEST


def norm_fwd(values, gain, shift):
    center = values - jnp.mean(values, -1, keepdims=True)
    inverse = lax.rsqrt(jnp.mean(center * center, -1, keepdims=True) + EPSILON)
    normed = center * inverse
    return (normed * gain + shift, normed, inverse)


def norm_back(grad, normed, inverse, gain):
    scaled = grad * gain
    inner = (
        scaled
        - jnp.mean(scaled, -1, keepdims=True)
        - normed * jnp.mean(scaled * normed, -1, keepdims=True)
    )
    return (inverse * inner, jnp.sum(grad * normed, 0), jnp.sum(grad, 0))


def offsets(size):
    places = jnp.arange(size)
    index = places[:, None] - places[None, :] + size - 1
    return (index[:, :, None] == jnp.arange(2 * size - 1)[None, None, :]).astype(jnp.float32)


def along_rows(left, right):
    return lax.dot_general(
        left, right, (((0,), (0,)), ((), ())), preferred_element_type=jnp.float32
    )


def against(left, right):
    return lax.dot_general(
        left, right, (((1,), (1,)), ((), ())), preferred_element_type=jnp.float32
    )


def scores_of(query, key_low, valid, table_h, table_w):
    blocks, length, heads, depth = query.shape
    size = table_h.shape[0]
    base = jnp.einsum(
        "gqhd,gkhd->ghqk", query, key_low, preferred_element_type=jnp.float32
    ) * depth ** (-0.5)
    wide = query.astype(jnp.float32).reshape(blocks, size, size, heads, depth)
    bias_h = jnp.einsum("gachd,abd->ghacb", wide, table_h, precision=HIGH)
    bias_w = jnp.einsum("gachd,ced->ghace", wide, table_w, precision=HIGH)
    total = (
        base.reshape(blocks, heads, size, size, size, size)
        + bias_h[..., :, None]
        + bias_w[..., None, :]
    )
    total = total.reshape(blocks, heads, length, length)
    return (jnp.where(valid[:, None, None, :] > 0, total, NEGATIVE), wide)


def attend(inputs, table_h, table_w):
    query, key_low, value, valid = inputs
    scores, wide = scores_of(query, key_low, valid, table_h, table_w)
    top = jnp.max(scores, -1, keepdims=True)
    expo = jnp.exp(scores - top)
    total = jnp.sum(expo, -1, keepdims=True)
    weights = (expo / total).astype(jnp.bfloat16)
    mixed = jnp.einsum("ghqk,gkhd->gqhd", weights, value, preferred_element_type=jnp.float32)
    return (mixed.astype(jnp.bfloat16), (top + jnp.log(total))[..., 0])


def attend_back(carry, inputs, table_h, table_w):
    query, key_low, value, valid, logsum, grad_mixed = inputs
    scores, wide = scores_of(query, key_low, valid, table_h, table_w)
    blocks, length, heads, depth = query.shape
    size = table_h.shape[0]
    scale = depth ** (-0.5)
    prob = jnp.exp(scores - logsum[..., None])
    grad_prob = jnp.einsum("gqhd,gkhd->ghqk", grad_mixed, value, preferred_element_type=jnp.float32)
    grad_value = jnp.einsum(
        "ghqk,gqhd->gkhd", prob.astype(jnp.bfloat16), grad_mixed, preferred_element_type=jnp.float32
    )
    delta = jnp.sum(prob * grad_prob, -1, keepdims=True)
    grad_scores = (prob * (grad_prob - delta)).astype(jnp.bfloat16)
    grad_query = (
        jnp.einsum("ghqk,gkhd->gqhd", grad_scores, key_low, preferred_element_type=jnp.float32)
        * scale
    )
    grad_key = (
        jnp.einsum("ghqk,gqhd->gkhd", grad_scores, query, preferred_element_type=jnp.float32)
        * scale
    )
    split = grad_scores.astype(jnp.float32).reshape(blocks, heads, size, size, size, size)
    grad_h = jnp.sum(split, -1)
    grad_w = jnp.sum(split, -2)
    extra = jnp.einsum("ghacb,abd->gachd", grad_h, table_h, precision=HIGH) + jnp.einsum(
        "ghace,ced->gachd", grad_w, table_w, precision=HIGH
    )
    grad_query = grad_query + extra.reshape(blocks, length, heads, depth)
    sum_h = carry[0] + jnp.einsum("ghacb,gachd->abd", grad_h, wide, precision=HIGH)
    sum_w = carry[1] + jnp.einsum("ghace,gachd->ced", grad_w, wide, precision=HIGH)
    return ((sum_h, sum_w), (grad_query, grad_key, grad_value))


def shards(
    block_input,
    cotangent,
    pad_mask,
    slot_window,
    qkv_w,
    proj_w,
    fc1_w,
    fc2_w,
    norm1_gain,
    norm1_bias,
    q_bias,
    v_bias,
    rel_h,
    rel_w,
    proj_bias,
    norm2_gain,
    norm2_bias,
    fc1_bias,
    fc2_bias,
):
    part = lax.axis_index("tensor")
    slots_all = slot_window.shape[0]
    length = pad_mask.shape[1]
    local_rows = block_input.shape[0]
    size = rel_h.shape[0] // 2 + 1
    live_all = jnp.repeat((slot_window >= 0).astype(jnp.float32), length)
    live = lax.dynamic_slice_in_dim(live_all, part * local_rows, local_rows)[:, None]
    w_qkv, w_proj, w_up, w_down = (
        lax.all_gather(qkv_w, "dp", axis=1, tiled=True),
        lax.all_gather(proj_w, "dp", axis=1, tiled=True),
        lax.all_gather(fc1_w, "dp", axis=0, tiled=True),
        lax.all_gather(fc2_w, "dp", axis=1, tiled=True),
    )
    heads_width = w_qkv.shape[2]
    hidden_width = w_up.shape[1]
    heads_local = heads_width // HD
    per_block = 4
    count = slots_all // per_block
    group_rows = slots_all * length
    block_shape = (count, per_block, length, heads_local, HD)
    alive = (slot_window >= 0).astype(jnp.int32)
    valid = jnp.take(pad_mask, jnp.maximum(slot_window, 0), axis=0) * alive[:, None]
    onehot = offsets(size)
    table_h = jnp.einsum("abk,kd->abd", onehot, rel_h, precision=HIGH)
    table_w = jnp.einsum("abk,kd->abd", onehot, rel_w, precision=HIGH)
    bias_q = lax.dynamic_slice_in_dim(q_bias, part * heads_width, heads_width)
    bias_v = lax.dynamic_slice_in_dim(v_bias, part * heads_width, heads_width)
    bias_up = lax.dynamic_slice_in_dim(fc1_bias, part * hidden_width, hidden_width)
    wide_x = block_input.astype(jnp.float32)
    normal1, normed1, inverse1 = norm_fwd(wide_x, norm1_gain, norm1_bias)
    rows1 = lax.all_gather(normal1.astype(jnp.bfloat16), "tensor", axis=0, tiled=True)
    query = (jnp.dot(rows1, w_qkv[0], preferred_element_type=jnp.float32) + bias_q).astype(
        jnp.bfloat16
    )
    key_low = jnp.dot(rows1, w_qkv[1], preferred_element_type=jnp.float32).astype(jnp.bfloat16)
    value = (jnp.dot(rows1, w_qkv[2], preferred_element_type=jnp.float32) + bias_v).astype(
        jnp.bfloat16
    )
    blocks_in = (
        query.reshape(block_shape),
        key_low.reshape(block_shape),
        value.reshape(block_shape),
        valid.reshape(count, per_block, length),
    )
    mixed, logsum = lax.map(partial(attend, table_h=table_h, table_w=table_w), blocks_in)
    mixed_rows = mixed.reshape(group_rows, heads_width)
    attn_branch = (
        lax.psum_scatter(
            jnp.dot(mixed_rows, w_proj, preferred_element_type=jnp.float32).astype(jnp.bfloat16),
            "tensor",
            scatter_dimension=0,
            tiled=True,
        ).astype(jnp.float32)
        + proj_bias
    )
    middle = wide_x + attn_branch
    normal2, normed2, inverse2 = norm_fwd(middle, norm2_gain, norm2_bias)
    rows2 = lax.all_gather(normal2.astype(jnp.bfloat16), "tensor", axis=0, tiled=True)
    upper = jnp.dot(rows2, w_up, preferred_element_type=jnp.float32) + bias_up
    active = jax.nn.gelu(upper, approximate=False).astype(jnp.bfloat16)
    mlp_branch = (
        lax.psum_scatter(
            jnp.dot(active, w_down, preferred_element_type=jnp.float32).astype(jnp.bfloat16),
            "tensor",
            scatter_dimension=0,
            tiled=True,
        ).astype(jnp.float32)
        + fc2_bias
    )
    result = ((middle + mlp_branch) * live).astype(jnp.bfloat16)
    w_qkv, w_proj, w_up, w_down = (
        lax.all_gather(qkv_w, "dp", axis=1, tiled=True),
        lax.all_gather(proj_w, "dp", axis=1, tiled=True),
        lax.all_gather(fc1_w, "dp", axis=0, tiled=True),
        lax.all_gather(fc2_w, "dp", axis=1, tiled=True),
    )
    grad_y = cotangent.astype(jnp.float32) * live
    grad_rows2 = lax.all_gather(grad_y.astype(jnp.bfloat16), "tensor", axis=0, tiled=True)
    grad_down = along_rows(active, grad_rows2)
    grad_active = against(grad_rows2, w_down)
    ignored, pull = jax.vjp(partial(jax.nn.gelu, approximate=False), upper)
    grad_upper = pull(grad_active)[0].astype(jnp.bfloat16)
    grad_up = along_rows(rows2, grad_upper)
    back2 = lax.psum_scatter(
        against(grad_upper, w_up).astype(jnp.bfloat16), "tensor", scatter_dimension=0, tiled=True
    ).astype(jnp.float32)
    grad_norm2, gain2_grad, shift2_grad = norm_back(back2, normed2, inverse2, norm2_gain)
    grad_middle = grad_y + grad_norm2
    grad_middle_low = grad_middle.astype(jnp.bfloat16)
    grad_rows1 = lax.all_gather(grad_middle_low, "tensor", axis=0, tiled=True)
    grad_proj = along_rows(mixed_rows, grad_rows1)
    grad_mixed = against(grad_rows1, w_proj).astype(jnp.bfloat16)
    zero_table = jnp.zeros_like(table_h)
    (rel_grad_h, rel_grad_w), (grad_query, grad_key, grad_value) = lax.scan(
        partial(attend_back, table_h=table_h, table_w=table_w),
        (zero_table, zero_table),
        blocks_in + (logsum, grad_mixed.reshape(block_shape)),
    )
    grads_low = [
        piece.reshape(group_rows, heads_width).astype(jnp.bfloat16)
        for piece in (grad_query, grad_key, grad_value)
    ]
    grad_qkv = jnp.stack([along_rows(rows1, piece) for piece in grads_low])
    back1 = (
        against(grads_low[0], w_qkv[0])
        + against(grads_low[1], w_qkv[1])
        + against(grads_low[2], w_qkv[2])
    )
    back1 = lax.psum_scatter(
        back1.astype(jnp.bfloat16), "tensor", scatter_dimension=0, tiled=True
    ).astype(jnp.float32)
    grad_norm1, gain1_grad, shift1_grad = norm_back(back1, normed1, inverse1, norm1_gain)
    grad_x = (grad_middle + grad_norm1).astype(jnp.bfloat16)
    full_q = lax.dynamic_update_slice_in_dim(
        jnp.zeros_like(q_bias), jnp.sum(grads_low[0], 0, dtype=jnp.float32), part * heads_width, 0
    )
    full_v = lax.dynamic_update_slice_in_dim(
        jnp.zeros_like(v_bias), jnp.sum(grads_low[2], 0, dtype=jnp.float32), part * heads_width, 0
    )
    full_up = lax.dynamic_update_slice_in_dim(
        jnp.zeros_like(fc1_bias), jnp.sum(grad_upper, 0, dtype=jnp.float32), part * hidden_width, 0
    )
    rel_h_grad = jnp.einsum("abk,abd->kd", onehot, rel_grad_h, precision=HIGH)
    rel_w_grad = jnp.einsum("abk,abd->kd", onehot, rel_grad_w, precision=HIGH)
    proj_bias_grad = jnp.sum(grad_middle_low, 0, dtype=jnp.float32)
    fc2_bias_grad = jnp.sum(grad_y, 0)
    small = lax.psum(
        (
            gain1_grad,
            shift1_grad,
            full_q,
            full_v,
            rel_h_grad,
            rel_w_grad,
            proj_bias_grad,
            gain2_grad,
            shift2_grad,
            full_up,
            fc2_bias_grad,
        ),
        ("dp", "tensor"),
    )
    attn_pair = (grad_qkv, grad_proj)
    mlp_pair = (grad_up, grad_down)
    weight_grads = (
        lax.psum_scatter(attn_pair[0], "dp", scatter_dimension=1, tiled=True),
        lax.psum_scatter(attn_pair[1], "dp", scatter_dimension=1, tiled=True),
        lax.psum_scatter(mlp_pair[0], "dp", scatter_dimension=0, tiled=True),
        lax.psum_scatter(mlp_pair[1], "dp", scatter_dimension=1, tiled=True),
    )
    return (
        result,
        grad_x,
        weight_grads[0],
        weight_grads[1],
        weight_grads[2],
        weight_grads[3],
        small[0],
        small[1],
        small[2],
        small[3],
        small[4],
        small[5],
        small[6],
        small[7],
        small[8],
        small[9],
        small[10],
    )


def solution(mesh):
    return jax.shard_map(
        shards,
        mesh=mesh,
        in_specs=(
            P(("dp", "tensor"), None),
            P(("dp", "tensor"), None),
            P(),
            P("dp"),
            P(None, "dp", "tensor"),
            P("tensor", "dp"),
            P("dp", "tensor"),
            P("tensor", "dp"),
            P(),
            P(),
            P(),
            P(),
            P(),
            P(),
            P(),
            P(),
            P(),
            P(),
            P(),
        ),
        out_specs=(
            P(("dp", "tensor"), None),
            P(("dp", "tensor"), None),
            P(None, "dp", "tensor"),
            P("tensor", "dp"),
            P("dp", "tensor"),
            P("tensor", "dp"),
            P(),
            P(),
            P(),
            P(),
            P(),
            P(),
            P(),
            P(),
            P(),
            P(),
            P(),
        ),
        check_vma=False,
    )
```

profile of v0, /device:TPU:1, one launch (start us, length us, event | category | flops | bytes accessed | tf_op | source)
XLA Modules:
  0.0 1463.3 jit_solution(7754894041037899018)
XLA Ops:
  16.4 27.8 %all_gather.30 = bf16[192,768]{0,1:T(8,128)(2,1)} all-gather(bf16[192,96]{0,1:T(8,128)(2,1)S(1)} %copy.132), channel_id=1, replica_groups=mesh['dp'=8,'tensor'=4] {'dp'}, dimensions={1}, use_global_device_ids=true | all-gather | bytes 331776 | tf_op jit(solution)/shard_map/all_gather | solution.py:143
  46.1 30.0 %all_gather.29 = bf16[3,768,192]{2,1,0:T(8,128)(2,1)S(1)} all-gather(bf16[3,96,192]{2,1,0:T(8,128)(2,1)S(1)} %copy-done.31), channel_id=1, replica_groups=mesh['dp'=8,'tensor'=4] {'dp'}, dimensions={1}, use_global_device_ids=true | all-gather | bytes 995328 | tf_op jit(solution)/shard_map/all_gather | solution.py:142
  115.5 242.9 %while.31 = (s32[]{:T(128)}, bf16[4,4,196,3,64]{2,1,0,4,3:T(4,128)(2,1)}, f32[4,4,3,196]{3,2,1,0:T(4,128)}, bf16[4,4,196,3,64]{2,4,3,1,0:T(8,128)(2,1)}, s32[4,4...) while((s32[]{:T(128)}, ...), condition=%wide.region_5.6_spmd, body=%wide.region_2.0_spmd.sunk | while | flops 173350240 | bytes 33403428 | solution.py:178
  131.1 12.7 add.381
  154.1 12.7 add.383
  191.7 12.7 add.381
  214.8 12.7 add.383
  252.4 12.7 add.381
  275.4 12.7 add.383
  313.0 12.7 add.381
  336.1 12.7 add.383
  366.7 59.2 %reduce-scatter.13.cloned.1.call-done = bf16[784,768]{1,0:T(8,128)(2,1)} async-done(((bf16[3136,768]{1,0:T(8,128)(2,1)}), bf16[784,768]{1,0:T(8,128)(2,1)}) %reduce-scatter.13.cloned.1.call-update) | async-done | bytes 1204240 | tf_op jit(solution)/shard_map/reduce_scatter | solution.py:181
  434.6 34.2 %all-gather.9.cloned.1.call-done = bf16[3136,768]{1,0:T(8,128)(2,1)} async-done(((bf16[784,768]{1,0:T(8,128)(2,1)}), bf16[3136,768]{1,0:T(8,128)(2,1)}) %all-gather.9.cloned.1.call-update) | async-done | bytes 4816912 | tf_op jit(solution)/shard_map/all_gather | solution.py:191
  479.2 31.2 %all-gather.13.cloned.1.call-done = bf16[768,768]{0,1:T(8,128)(2,1)} async-done(((bf16[768,96]{0,1:T(8,128)(2,1)}), bf16[768,768]{0,1:T(8,128)(2,1)}) %all-gather.13.cloned.1.call-update) | async-done | bytes 1179664 | tf_op jit(solution)/shard_map/all_gather | solution.py:145
  510.3 40.4 %all-gather.15.cloned.1.call-done = bf16[3136,768]{1,0:T(8,128)(2,1)} async-done(((bf16[784,768]{1,0:T(8,128)(2,1)}), bf16[3136,768]{1,0:T(8,128)(2,1)}) %all-gather.15.cloned.1.call-update) | async-done | bytes 4816912 | tf_op jit(solution)/shard_map/all_gather | solution.py:211
  550.7 29.8 %convert_reduce_fusion = (f32[768]{0:T(1024)}, bf16[3136,768]{1,0:T(8,128)(2,1)S(1)}, f32[3136,768]{1,0:T(8,128)}) fusion(f32[3136,768]{1,0:T(8,128)} %fusion.105, f32[768]{0:T(1024)S(1)} %dynamic_slice.47, bf16[3136,768]{1,0:T(8,128)(2,1)} %all-gather.15.cloned.1.call-done, bf16[768,768]{0,1:T(8,128)(2,1)} %all-gather.13.cloned.1.call-done), kind=kOutput, calls=%fused_computation.80 | convolution fusion | flops 3880008960 | bytes 30087168 | tf_op jit(solution)/shard_map/dot_general | solution.py:46
  608.8 27.7 %reduce-scatter.17.cloned.1.call-done = bf16[784,768]{1,0:T(8,128)(2,1)} async-done(((bf16[3136,768]{1,0:T(8,128)(2,1)}), bf16[784,768]{1,0:T(8,128)(2,1)}) %reduce-scatter.17.cloned.1.call-update) | async-done | bytes 1204240 | tf_op jit(solution)/shard_map/reduce_scatter | solution.py:217
  639.9 47.7 %reduce-scatter.15.cloned.1.call-done = bf16[784,768]{1,0:T(8,128)(2,1)} async-done(((bf16[3136,768]{1,0:T(8,128)(2,1)}), bf16[784,768]{1,0:T(8,128)(2,1)}) %reduce-scatter.15.cloned.1.call-update) | async-done | bytes 1204240 | tf_op jit(solution)/shard_map/reduce_scatter | solution.py:195
  693.7 38.4 %all-gather.17.cloned.1.call-done = bf16[3136,768]{1,0:T(8,128)(2,1)} async-done(((bf16[784,768]{1,0:T(8,128)(2,1)}), bf16[3136,768]{1,0:T(8,128)(2,1)}) %all-gather.17.cloned.1.call-update) | async-done | bytes 4816912 | tf_op jit(solution)/shard_map/all_gather | solution.py:223
  747.6 411.3 %while.32 = (s32[]{:T(128)}, f32[14,14,64]{2,1,0:T(8,128)}, f32[14,14,64]{2,1,0:T(8,128)}, bf16[4,4,196,3,64]{2,4,3,1,0:T(8,128)(2,1)}, bf16[4,4,196,3,64]{2,4,3...) while((s32[]{:T(128)}, f32[14,14,64]{2,1,0:T(8,128)}, ...), condition=%wide.region_17.18_spmd.clone, body=%wide.region_13.17_spmd.clone.sunk | while | flops 453344864 | bytes 81278464 | solution.py:227
  767.3 12.7 add.390
  791.4 12.7 add.392
  870.1 12.7 add.390
  894.1 12.7 add.392
  972.8 12.7 add.390
  996.8 12.7 add.392
  1099.5 12.7 add.392
  1228.9 29.8 %reduce-scatter.25.cloned.1.call-done = f32[96,576]{1,0:T(8,128)} async-done(((f32[768,576]{1,0:T(8,128)}), f32[96,576]{1,0:T(8,128)}) %reduce-scatter.25.cloned.1.call-update) | async-done | bytes 221200
  1260.6 49.0 %reduce-scatter.19.cloned.1.call-done = bf16[784,768]{1,0:T(8,128)(2,1)} async-done(((bf16[3136,768]{1,0:T(8,128)(2,1)}), bf16[784,768]{1,0:T(8,128)(2,1)}) %reduce-scatter.19.cloned.1.call-update) | async-done | bytes 1204240 | tf_op jit(solution)/shard_map/reduce_scatter | solution.py:242
  1312.2 42.1 %all-reduce = (f32[768]{0:T(1024)}, f32[768]{0:T(1024)}, f32[768]{0:T(1024)}, f32[768]{0:T(1024)}, f32[27,64]{1,0:T(8,128)}, /*index=5*/f32[27,64]{1,0:T(8,128)}...) all-reduce(f32[768]{0:T(1024)S(1)} %get-tuple-element.317, ...), channel_id=1, replica_groups=mesh['dp'=8,'tensor'=4] {'dp','tensor'}, use_global_device_ids=true, to_apply=%region_26.27 | all-reduce | flops 12672 | bytes 101376 | tf_op jit(solution)/shard_map/psum | solution.py:260
  1357.4 25.2 %reduce-scatter.23.cloned.1.call-done = f32[768,96]{0,1:T(8,128)} async-done(((f32[768,768]{0,1:T(8,128)}), f32[768,96]{0,1:T(8,128)}) %reduce-scatter.23.cloned.1.call-update) | async-done | bytes 294928 | tf_op jit(solution)/shard_map/reduce_scatter | solution.py:282
  1382.6 73.4 %reduce-scatter.21.cloned.1.call-done = f32[96,768]{1,0:T(8,128)} async-done(((f32[768,768]{1,0:T(8,128)}), f32[96,768]{1,0:T(8,128)}) %reduce-scatter.21.cloned.1.call-update) | async-done | bytes 294928 | tf_op jit(solution)/shard_map/reduce_scatter | solution.py:281
  (472 shorter events, 669.6 us)
Async XLA Ops:
  8.0 36.3 %copy-start = (f32[27,64]{1,0:T(8,128)S(1)}, f32[27,64]{1,0:T(8,128)}, u32[]{:S(2)}) copy-start(f32[27,64]{1,0:T(8,128)} %param.36) | copy-start | bytes 20740
  8.1 68.0 %all-gather.7.cloned.1.call-start = ((), (), s32[]{:S(2)}) async-start(), calls=%async_computation.8 | async-start | bytes 6021120 | tf_op jit(solution)/shard_map/all_gather | solution.py:164
  11.6 33.6 %copy-start.46 = (f32[27,64]{1,0:T(8,128)S(1)}, f32[27,64]{1,0:T(8,128)}, u32[]{:S(2)}) copy-start(f32[27,64]{1,0:T(8,128)} %param.35) | copy-start | bytes 20740
  11.7 34.4 %copy-start.31 = (bf16[3,96,192]{2,1,0:T(8,128)(2,1)S(1)}, bf16[3,96,192]{2,1,0:T(8,128)(2,1)}, u32[]{:S(2)}) copy-start(bf16[3,96,192]{2,1,0:T(8,128)(2,1)} %param.27) | copy-start | bytes 331780
  13.3 412.7 %reduce-scatter.13.cloned.1.call-start = ((), (), s32[]{:S(2)}) async-start(), calls=%async_computation.9 | async-start | bytes 6021120 | tf_op jit(solution)/shard_map/reduce_scatter | solution.py:181
  366.0 59.9 %copy-start.5 = (bf16[784,768]{1,0:T(8,128)(2,1)S(1)}, bf16[784,768]{1,0:T(8,128)(2,1)}, u32[]{:S(2)}) copy-start(bf16[784,768]{1,0:T(8,128)(2,1)} %param.23) | copy-start | bytes 3612676
  366.0 59.9 %copy-start.35 = (f32[768]{0:T(1024)S(1)}, f32[768]{0:T(1024)}, u32[]{:S(2)}) copy-start(f32[768]{0:T(1024)} %param.37) | copy-start | bytes 9220
  366.0 68.5 %all-gather.11.cloned.1.call-start = ((), (), s32[]{:S(2)}) async-start(), calls=%async_computation.11 | async-start | bytes 1327104 | tf_op jit(solution)/shard_map/all_gather | solution.py:144
  366.6 61.9 %copy-start.41 = (f32[768]{0:T(1024)S(1)}, f32[768]{0:T(1024)}, u32[]{:S(2)}) copy-start(f32[768]{0:T(1024)} %param.38) | copy-start | bytes 9220
  366.6 61.9 %copy-start.50 = (f32[768]{0:T(1024)S(1)}, f32[768]{0:T(1024)}, u32[]{:S(2)}) copy-start(f32[768]{0:T(1024)} %param.39) | copy-start | bytes 9220
  366.6 102.2 %all-gather.9.cloned.1.call-start = ((), (), s32[]{:S(2)}) async-start(), calls=%async_computation.10 | async-start | bytes 6021120 | tf_op jit(solution)/shard_map/all_gather | solution.py:191
  430.3 80.0 %all-gather.13.cloned.1.call-start = ((), (), s32[]{:S(2)}) async-start(), calls=%async_computation.12 | async-start | bytes 1327104 | tf_op jit(solution)/shard_map/all_gather | solution.py:145
  430.9 119.8 %all-gather.15.cloned.1.call-start = ((), (), s32[]{:S(2)}) async-start(), calls=%async_computation.14 | async-start | bytes 6021120 | tf_op jit(solution)/shard_map/all_gather | solution.py:211
  433.8 202.8 %reduce-scatter.17.cloned.1.call-start = ((), (), s32[]{:S(2)}) async-start(), calls=%async_computation.15 | async-start | bytes 6021120 | tf_op jit(solution)/shard_map/reduce_scatter | solution.py:217
  588.4 99.2 %reduce-scatter.15.cloned.1.call-start = ((), (), s32[]{:S(2)}) async-start(), calls=%async_computation.13 | async-start | bytes 6021120 | tf_op jit(solution)/shard_map/reduce_scatter | solution.py:195
  608.7 78.8 %copy-start.48 = (f32[768]{0:T(1024)S(1)}, f32[768]{0:T(1024)}, u32[]{:S(2)}) copy-start(f32[768]{0:T(1024)} %param.41) | copy-start | bytes 9220
  608.7 123.4 %all-gather.17.cloned.1.call-start = ((), (), s32[]{:S(2)}) async-start(), calls=%async_computation.16 | async-start | bytes 6021120 | tf_op jit(solution)/shard_map/all_gather | solution.py:223
  693.6 533.6 %reduce-scatter.27.cloned.1.call-start = ((), (), s32[]{:S(2)}) async-start(), calls=%async_computation.21 | async-start | bytes 884736
  737.9 520.8 %reduce-scatter.25.cloned.1.call-start = ((), (), s32[]{:S(2)}) async-start(), calls=%async_computation.20 | async-start | bytes 2211840
  1192.5 117.1 %reduce-scatter.19.cloned.1.call-start = ((), (), s32[]{:S(2)}) async-start(), calls=%async_computation.17 | async-start | bytes 6021120 | tf_op jit(solution)/shard_map/reduce_scatter | solution.py:242
  1203.1 179.5 %reduce-scatter.23.cloned.1.call-start = ((), (), s32[]{:S(2)}) async-start(), calls=%async_computation.19 | async-start | bytes 2654208 | tf_op jit(solution)/shard_map/reduce_scatter | solution.py:282
  1212.6 243.4 %reduce-scatter.21.cloned.1.call-start = ((), (), s32[]{:S(2)}) async-start(), calls=%async_computation.18 | async-start | bytes 2654208 | tf_op jit(solution)/shard_map/reduce_scatter | solution.py:281
  1223.8 85.8 %copy-start.6 = (bf16[784,768]{1,0:T(8,128)(2,1)S(1)}, bf16[784,768]{1,0:T(8,128)(2,1)}, u32[]{:S(2)}) copy-start(bf16[784,768]{1,0:T(8,128)(2,1)} %param.23) | copy-start | bytes 3612676
  1223.8 85.8 %copy-start.33 = (f32[784]{0:T(1024)S(1)}, f32[784]{0:T(1024)}, u32[]{:S(2)}) copy-start(f32[784]{0:T(1024)} %copy-done.32) | copy-start | bytes 9412
  1223.8 85.8 %copy-start.37 = (f32[784]{0:T(1024)S(1)}, f32[784]{0:T(1024)}, u32[]{:S(2)}) copy-start(f32[784]{0:T(1024)} %copy-done.36) | copy-start | bytes 9412
  1223.8 85.8 %copy-start.40 = (f32[768]{0:T(1024)S(1)}, f32[768]{0:T(1024)}, u32[]{:S(2)}) copy-start(f32[768]{0:T(1024)} %param.31) | copy-start | bytes 9220
  1226.0 86.1 %copy-start.42 = (f32[768]{0:T(1024)S(1)}, f32[768]{0:T(1024)}, u32[]{:S(2)}) copy-start(f32[768]{0:T(1024)} %get-tuple-element.315) | copy-start | bytes 9220
  1226.0 86.1 %copy-start.43 = (f32[768]{0:T(1024)S(1)}, f32[768]{0:T(1024)}, u32[]{:S(2)}) copy-start(f32[768]{0:T(1024)} %get-tuple-element.321) | copy-start | bytes 9220
  1226.0 86.2 %copy-start.44 = (f32[768]{0:T(1024)S(1)}, f32[768]{0:T(1024)}, u32[]{:S(2)}) copy-start(f32[768]{0:T(1024)} %get-tuple-element.383) | copy-start | bytes 9220
  1226.0 86.2 %copy-start.45 = (f32[768]{0:T(1024)S(1)}, f32[768]{0:T(1024)}, u32[]{:S(2)}) copy-start(f32[768]{0:T(1024)} %get-tuple-element.391) | copy-start | bytes 9220
  1309.6 44.7 %copy-start.21 = (bf16[784,768]{1,0:T(8,128)(2,1)S(1)}, bf16[784,768]{1,0:T(8,128)(2,1)}, u32[]{:S(2)}) copy-start(bf16[784,768]{1,0:T(8,128)(2,1)} %reduce-scatter.19.cloned.1.call-done) | copy-start | bytes 3612676
  1354.3 101.7 %copy-start.1 = (f32[27,64]{1,0:T(8,128)S(1)}, f32[27,64]{1,0:T(8,128)}, u32[]{:S(2)}) copy-start(f32[27,64]{1,0:T(8,128)} %param.36) | copy-start | bytes 20740
  (67 other events, 363.8 us)
Sparse Core Ops, SparseCore 0:
  13.4 40.4 all-gather.6
  366.2 59.7 reduce-scatter.12
  588.5 48.0 reduce-scatter.16
  639.0 48.5 reduce-scatter.14
Sparse Core Ops, SparseCore 1:
  368.7 51.0 all-gather.10
  430.4 38.4 all-gather.8
  470.9 39.4 all-gather.12
  512.5 38.2 all-gather.14
  693.7 38.4 all-gather.16
  738.0 61.0 reduce-scatter.26
  1192.6 66.1 reduce-scatter.24
  1261.1 48.4 reduce-scatter.18
  1313.5 69.0 reduce-scatter.22
  1386.7 69.2 reduce-scatter.20
where the time goes:
time: 1470 us; the launch traced here: 1460 us
  local copies, waits for them, and re-layouts  566 us (39%)
  waiting for transfers between devices  457 us (31%)
  matrix products  235 us (16%)
  blocking collectives  99.9 us (7%)
  other arithmetic  85.9 us (6%)
  between operations  16.3 us (1%)
    add x48, local copies, waits for them, and re-layouts, scores_of(): base.reshape(blocks, heads, size, size, size, size) + bias_h[..., :, None]  381 us
    reduce_scatter x1, waiting for transfers between devices, shards(): lax.psum_scatter(mlp_pair[0], 'dp', scatter_dimension=0, tiled=True)  73.4 us
    reduce_scatter x1, waiting for transfers between devices, shards(): lax.psum_scatter(jnp.dot(mixed_rows, w_proj, preferred_element_type=jnp.f...  59.2 us
    reshape x8, local copies, waits for them, and re-layouts, attend_back(): grad_scores.astype(jnp.float32)  53.6 us
    reduce_scatter x1, waiting for transfers between devices, shards(): lax.psum_scatter(back1.astype(jnp.bfloat16), 'tensor', scatter_dimension=...  49 us
    dot_general x6, matrix products, against(): lax.dot_general(left, right, (((1,), (1,)), ((), ())), preferred_element_...  48.7 us
    reduce_scatter x1, waiting for transfers between devices, shards(): lax.psum_scatter(jnp.dot(active, w_down, preferred_element_type=jnp.float...  47.7 us
    psum x1, blocking collectives, shards(): lax.psum((gain1_grad, shift1_grad, full_q, full_v, rel_h_grad, rel_w_grad...  42.1 us
  transfers between devices with their start and end apart: 14, of which 11 were waited for; matrix products, arithmetic and copies ran while one was open for 36% of the time, Pallas kernels for 0%

commit v1 on v0

v1 whole, which is shorter than its diff:
```python
from functools import partial

import jax
import jax.numpy as jnp
import numpy as np
from jax import lax
from jax.experimental import pallas as pl
from jax.experimental.pallas import tpu as pltpu
from jax.sharding import PartitionSpec as P

HD = 64
EPSILON = 1e-06
NEGATIVE = -1e30
F32, BF = jnp.float32, jnp.bfloat16
AXES = ("dp", "tensor")
VMEM_LIMIT = 60 * 1024 * 1024


def nn(left, right):
    return lax.dot_general(left, right, (((1,), (0,)), ((), ())), preferred_element_type=F32)


def nt(left, right):
    return lax.dot_general(left, right, (((1,), (1,)), ((), ())), preferred_element_type=F32)


def tn(left, right):
    return lax.dot_general(left, right, (((0,), (0,)), ((), ())), preferred_element_type=F32)


def normed_of(values):
    center = values - jnp.mean(values, -1, keepdims=True)
    inverse = lax.rsqrt(jnp.mean(center * center, -1, keepdims=True) + EPSILON)
    return center * inverse, inverse


def norm_back(grad, normed, inverse, gain):
    scaled = grad * gain
    inner = (
        scaled
        - jnp.mean(scaled, -1, keepdims=True)
        - normed * jnp.mean(scaled * normed, -1, keepdims=True)
    )
    return inverse * inner


def lanes_of(shape):
    return lax.broadcasted_iota(jnp.int32, shape, 1)


def shift_lanes(values, amounts, left):
    for bit in (1, 2, 4, 8):
        moved = pltpu.roll(values, 128 - bit if left else bit, 1)
        values = jnp.where((amounts & bit) != 0, moved, values)
    return values


def attend_kernel(
    x_ref, wa_ref, wb_ref, gain_ref, shift_ref, bias_ref, table_ref, key_feat_ref, amount_ref,
    query_ref, key_ref, value_ref, out_ref, acc_ref, h1_ref, qk_ref, vv_ref,
    *, windows, padded, keys,
):
    step = pl.program_id(0)

    @pl.when(step == 0)
    def _():
        normed, _ = normed_of(x_ref[...].astype(F32))
        h1_ref[...] = (normed * gain_ref[...] + shift_ref[...]).astype(BF)
        acc_ref[...] = jnp.zeros_like(acc_ref)

    h1 = h1_ref[...]
    qk_ref[...] = (nn(h1, wa_ref[...]) + bias_ref[0:1, :384]).astype(BF)
    vv_ref[...] = (nn(h1, wb_ref[:, :256]) + bias_ref[0:1, 384:640]).astype(BF)
    lane = lanes_of((padded, 128))
    low = lane < 64
    field = lane & 31
    amounts = amount_ref[...]
    pad_lane = lanes_of((keys - padded, 128))
    pad_key = jnp.where(pad_lane == 79, NEGATIVE, 0.0).astype(BF)

    def window(w, carry):
        rows = pl.ds(pl.multiple_of(w * padded, 16), padded)
        qk = qk_ref[rows, :]
        vv = vv_ref[rows, :]
        spread = nn(qk[:, :256], table_ref[0]) + nn(qk[:, :256], table_ref[1])
        wide = qk.astype(F32)
        wide_v = vv.astype(F32)
        parts = [wide[:, :128], wide[:, 128:256], wide[:, 256:384]]
        turned = [pltpu.roll(part, 64, 1) for part in parts]
        queries = [parts[0], turned[0], parts[1]]
        keys_low = [turned[1], parts[2], turned[2]]
        values = [wide_v[:, :128], pltpu.roll(wide_v[:, :128], 64, 1), wide_v[:, 128:256]]
        key_feat = key_feat_ref[rows, :].astype(F32)
        ones = jnp.where((lane == 64) | (lane == 65), 1.0, 0.0)
        outs = []
        for head in range(3):
            moved = shift_lanes(spread[:, head * 128 : head * 128 + 128], amounts, True)
            high = moved.astype(BF).astype(F32)
            rest = pltpu.roll(moved - high, 16, 1)
            feat = jnp.where(field < 16, high, rest)
            feat = jnp.where(field < 14, feat, jnp.where((field >= 16) & (field < 30), feat, 0.0))
            feat = jnp.where(lane == 79, 1.0, feat)
            query = jnp.where(low, queries[head] * 0.125, feat)
            key_ref[0, head, w, :padded, :] = jnp.where(low, keys_low[head], key_feat).astype(BF)
            key_ref[0, head, w, padded:, :] = pad_key
            value_ref[0, head, w, :padded, :] = jnp.where(low, values[head], ones).astype(BF)
            value_ref[0, head, w, padded:, :] = jnp.zeros((keys - padded, 128), BF)
            scores = nt(query.astype(BF), key_ref[0, head, w])
            top = jnp.max(scores, -1, keepdims=True)
            expo = jnp.exp(scores - top).astype(BF)
            mixed = nn(expo, value_ref[0, head, w])
            total = mixed[:, 64:65]
            outs.append(mixed / total)
            logsum = -(top + jnp.log(total))
            first = logsum.astype(BF).astype(F32)
            second = (logsum - first).astype(BF).astype(F32)
            third = logsum - first - second
            query = jnp.where(lane == 78, first, query)
            query = jnp.where(lane == 94, second, query)
            query = jnp.where(lane == 95, third, query)
            query_ref[0, head, rows, :] = query.astype(BF)
        out_ref[0, rows, :128] = jnp.where(low, 0.0, pltpu.roll(outs[0], 64, 1)).astype(BF)
        out_ref[0, rows, 128:] = jnp.where(low, outs[1], pltpu.roll(outs[2], 64, 1)).astype(BF)
        return carry

    lax.fori_loop(0, windows, window, 0)
    acc_ref[...] += nt(out_ref[0], wb_ref[:, 128:])


def mlp_kernel(
    x_ref, attn_ref, gy_ref, live_ref, up_ref, down_ref, bias_up_ref, gain_ref, shift_ref, bias_proj_ref, bias_down_ref,
    result_ref, gx1_ref, grad_up_ref, grad_down_ref, gbias_up_ref, small_ref,
    x1_ref, h2_ref, h2t_ref, gyt_ref, y_ref, dh_ref,
):
    step = pl.program_id(0)
    last = pl.num_programs(0) - 1

    @pl.when(step == 0)
    def _():
        x1 = x_ref[...].astype(F32) + (attn_ref[...] + bias_proj_ref[...])
        x1_ref[...] = x1
        normed, _ = normed_of(x1)
        h2 = (normed * gain_ref[...] + shift_ref[...]).astype(BF)
        h2_ref[...] = h2
        h2t_ref[...] = h2.T
        gyt_ref[...] = gy_ref[...].T
        y_ref[...] = jnp.zeros_like(y_ref)
        dh_ref[...] = jnp.zeros_like(dh_ref)

    up, down = up_ref[...], down_ref[...]
    upper = nn(h2_ref[...], up) + bias_up_ref[0]
    half = 0.5 * (1.0 + lax.erf(upper * np.float32(np.sqrt(0.5))))
    slope = half + upper * (np.float32(1.0 / np.sqrt(2 * np.pi)) * jnp.exp(-0.5 * upper * upper))
    active = (upper * half).astype(BF)
    grad_upper = (nn(gy_ref[...], down) * slope).astype(BF)
    y_ref[...] += nt(active, down)
    dh_ref[...] += nt(grad_upper, up)
    grad_down_ref[0] = nn(gyt_ref[...], active).astype(grad_down_ref.dtype)
    grad_up_ref[0] = nn(h2t_ref[...], grad_upper).astype(grad_up_ref.dtype)
    gbias_up_ref[0] = jnp.sum(grad_upper.astype(F32), 0, keepdims=True)

    @pl.when(step == last)
    def _():
        x1 = x1_ref[...]
        result = live_ref[...][:, :1] * (x1 + (y_ref[...] + bias_down_ref[...]))
        result_ref[...] = result.astype(BF)
        normed, inverse = normed_of(x1)
        gy = gy_ref[...].astype(F32)
        dh = dh_ref[...]
        gx1_ref[...] = gy + norm_back(dh, normed, inverse, gain_ref[...])
        small_ref[0:1, :] = jnp.sum(dh * normed, 0, keepdims=True)
        small_ref[1:2, :] = jnp.sum(dh, 0, keepdims=True)
        small_ref[2:3, :] = jnp.sum(gy, 0, keepdims=True)
        small_ref[3:8, :] = jnp.zeros_like(small_ref[3:8, :])


def attend_back_kernel(
    x_ref, gx1_ref, wa_ref, wb_ref, gain_ref, shift_ref, table_ref, amount_ref,
    query_ref, key_ref, value_ref, out_ref,
    grad_x_ref, grad_ref, small_ref, gbias_ref, grel_ref,
    h1t_ref, gbt_ref, gb_ref, dh_ref, do_ref, gqk_ref, gv_ref, spread_ref,
    *, windows, padded, keys,
):
    step = pl.program_id(0)
    last = pl.num_programs(0) - 1

    @pl.when(step == 0)
    def _():
        normed, _ = normed_of(x_ref[...].astype(F32))
        h1t_ref[...] = (normed * gain_ref[...] + shift_ref[...]).astype(BF).T
        gb = gx1_ref[...].astype(BF)
        gb_ref[...] = gb
        gbt_ref[...] = gb.T
        dh_ref[...] = jnp.zeros_like(dh_ref)
        grel_ref[...] = jnp.zeros_like(grel_ref)
        small_ref[0:1, :] = jnp.sum(gb.astype(F32), 0, keepdims=True)

    do_ref[...] = nn(gb_ref[...], wb_ref[:, 128:]).astype(BF)
    lane = lanes_of((padded, 128))
    low = lane < 64
    field = lane & 31
    amounts = amount_ref[...]
    kept = (lane >= 64) & (field < 14)

    def window(w, carry):
        rows = pl.ds(pl.multiple_of(w * padded, 16), padded)
        do = do_ref[rows, :].astype(F32)
        out = out_ref[0, rows, :].astype(F32)
        product = do * out
        grads = [pltpu.roll(do[:, :128], 64, 1), do[:, 128:], pltpu.roll(do[:, 128:], 64, 1)]
        sums = [
            jnp.sum(jnp.where(low, 0.0, product[:, :128]), -1, keepdims=True),
            jnp.sum(jnp.where(low, product[:, 128:], 0.0), -1, keepdims=True),
            jnp.sum(jnp.where(low, 0.0, product[:, 128:]), -1, keepdims=True),
        ]
        gq, gk, gv = [], [], []
        for head in range(3):
            delta = -sums[head]
            first = delta.astype(BF).astype(F32)
            grad_out = jnp.where(low, grads[head], jnp.where(lane == 64, first, jnp.where(lane == 65, delta - first, 0.0))).astype(BF)
            query, key, value = query_ref[0, head, rows, :], key_ref[0, head, w], value_ref[0, head, w]
            prob = jnp.exp(nt(query, key))
            grad_scores = (prob * nt(grad_out, value)).astype(BF)
            gv.append(tn(prob.astype(BF), grad_out)[:padded])
            gk.append(tn(grad_scores, query)[:padded])
            both = nn(grad_scores, key)
            back = shift_lanes(jnp.where(kept, both, 0.0), amounts, False)
            high = back.astype(BF).astype(F32)
            pack = jnp.where(low, pltpu.roll(back - high, 64, 1), high).astype(BF)
            spread_ref[head, rows, :] = pack
            gq.append(both * 0.125 + nn(pack, table_ref[...]))
        gqk_ref[rows, :128] = jnp.where(low, gq[0], pltpu.roll(gq[1], 64, 1)).astype(BF)
        gqk_ref[rows, 128:256] = jnp.where(low, gq[2], pltpu.roll(gk[0], 64, 1)).astype(BF)
        gqk_ref[rows, 256:] = jnp.where(low, gk[1], pltpu.roll(gk[2], 64, 1)).astype(BF)
        gv_ref[rows, :128] = jnp.where(low, gv[0], pltpu.roll(gv[1], 64, 1)).astype(BF)
        gv_ref[rows, 128:] = jnp.where(low, gv[2], 0.0).astype(BF)
        return carry

    lax.fori_loop(0, windows, window, 0)
    for head in range(3):
        grel_ref[...] += tn(spread_ref[head], query_ref[0, head])
    gqk, gv = gqk_ref[...], gv_ref[...]
    gbias_ref[0, :, :384] = jnp.sum(gqk.astype(F32), 0, keepdims=True)
    gbias_ref[0, :, 384:] = jnp.sum(gv.astype(F32), 0, keepdims=True)
    dh_ref[...] += nt(gqk, wa_ref[...]) + nt(gv, wb_ref[:, :256])
    h1t = h1t_ref[...]
    grad_ref[0, 0] = nn(h1t, gqk).astype(grad_ref.dtype)
    one, two = nn(h1t, gv), nn(gbt_ref[...], out_ref[0])
    grad_ref[0, 1, :, :128] = one[:, :128].astype(grad_ref.dtype)
    grad_ref[0, 1, :, 128:256] = (one[:, 128:] + two[:, :128]).astype(grad_ref.dtype)
    grad_ref[0, 1, :, 256:] = two[:, 128:].astype(grad_ref.dtype)

    @pl.when(step == last)
    def _():
        normed, inverse = normed_of(x_ref[...].astype(F32))
        dh = dh_ref[...]
        grad_x_ref[...] = (gx1_ref[...] + norm_back(dh, normed, inverse, gain_ref[...])).astype(BF)
        small_ref[1:2, :] = jnp.sum(dh * normed, 0, keepdims=True)
        small_ref[2:3, :] = jnp.sum(dh, 0, keepdims=True)
        small_ref[3:8, :] = jnp.zeros_like(small_ref[3:8, :])


def whole(shape):
    return pl.BlockSpec(shape, lambda *index: (0,) * len(shape))


def once(shape):
    return pl.BlockSpec(shape, lambda *index: (0,) * len(shape), pipeline_mode=pl.Buffered(1))


def shards(
    block_input, cotangent, pad_mask, slot_window, qkv_w, proj_w, fc1_w, fc2_w,
    norm1_gain, norm1_bias, q_bias, v_bias, rel_h, rel_w, proj_bias,
    norm2_gain, norm2_bias, fc1_bias, fc2_bias,
):
    part = lax.axis_index("tensor")
    count_dp, count_t = lax.axis_size("dp"), lax.axis_size("tensor")
    length = pad_mask.shape[1]
    local_rows, width = block_input.shape
    windows = local_rows // length
    size = rel_h.shape[0] // 2 + 1
    padded = -(-length // 16) * 16
    keys = -(-length // 128) * 128
    rows = windows * padded
    strip = width // count_dp

    mine = lax.dynamic_slice_in_dim(slot_window, part * windows, windows)
    alive = mine >= 0
    valid = jnp.take(pad_mask, jnp.maximum(mine, 0), axis=0)
    usable = (valid > 0) & alive[:, None]
    usable = jnp.pad(usable, ((0, 0), (0, padded - length)))
    mask = jnp.where(usable, 0.0, NEGATIVE).reshape(rows, 1)
    live = jnp.pad(jnp.broadcast_to(alive.astype(F32)[:, None], (windows, length)), ((0, 0), (0, padded - length)))
    live = jnp.broadcast_to(live.reshape(rows, 1), (rows, 128))

    def pad_rows(values):
        return jnp.pad(values.reshape(windows, length, width), ((0, 0), (0, padded - length), (0, 0))).reshape(rows, width)

    def cut_rows(values):
        return values.reshape(windows, padded, width)[:, :length].reshape(local_rows, width)

    x = pad_rows(block_input)
    gy = pad_rows(
        jnp.where(alive[:, None, None], cotangent.reshape(windows, length, width), jnp.zeros((), BF)).reshape(local_rows, width)
    )

    place = np.arange(padded)
    row_of, col_of = place // size, place % size
    inside = place < length
    amount = np.zeros((padded, 128), np.int32)
    amount[:, :] = np.where(
        (np.arange(128) % 64 < 32)[None, :], (size - 1 - row_of)[:, None], (size - 1 - col_of)[:, None]
    ) * inside[:, None]
    amount = jnp.asarray(amount)
    feat = np.zeros((padded, 128), np.float32)
    for a in range(size):
        for base, pos in ((64, row_of), (96, col_of)):
            feat[:, base + a] = (pos == a) & inside
            feat[:, base + 16 + a] = (pos == a) & inside
    feat[:, [78, 94, 95]] = 1.0
    key_feat = jnp.where(np.arange(128)[None, :] == 79, mask, jnp.tile(jnp.asarray(feat), (windows, 1))).astype(BF)

    span = rel_h.shape[0]
    table = jnp.zeros((64, HD), F32).at[:span].set(rel_h[::-1]).at[32 : 32 + span].set(rel_w[::-1])
    table_hi = table.astype(BF)
    table_lo = (table - table_hi.astype(F32)).astype(BF)

    def block_diag(piece):
        big = jnp.zeros((256, 384), BF)
        for head in range(3):
            big = big.at[head * 64 : head * 64 + 64, head * 128 + 64 : head * 128 + 128].set(piece.T)
        return big

    spread_table = jnp.stack([block_diag(table_hi), block_diag(table_lo)])
    back_table = jnp.zeros((128, 128), BF).at[:64, :64].set(table_hi).at[64:, :64].set(table_hi)

    q_w, k_w, v_w = qkv_w[0], qkv_w[1], qkv_w[2]
    shard = jnp.stack(
        [
            jnp.concatenate([q_w, k_w], 1),
            jnp.concatenate([v_w, proj_w.T], 1),
            fc1_w[:, :384],
            fc1_w[:, 384:],
            fc2_w.T[:, :384],
            fc2_w.T[:, 384:],
        ]
    )
    gathered_a = lax.all_gather(shard[:2], AXES, axis=0, tiled=False).reshape(count_dp, count_t, 2, strip, 384)
    gathered_m = lax.all_gather(shard[2:], AXES, axis=0, tiled=False).reshape(count_dp, count_t, 4, strip, 384)
    w_att = gathered_a.transpose(1, 2, 0, 3, 4).reshape(count_t, 2, width, 384)
    w_mlp = gathered_m.transpose(2, 1, 0, 3, 4).reshape(2, 2, count_t, width, 384).transpose(0, 2, 1, 3, 4)
    w_up = w_mlp[0].reshape(count_t * 2, width, 384)
    w_down = w_mlp[1].reshape(count_t * 2, width, 384)

    row = lambda v: v.reshape(1, -1)
    bias_att = jnp.zeros((count_t, 1, 640), F32)
    bias_att = bias_att.at[:, 0, :192].set(q_bias.reshape(count_t, 192)).at[:, 0, 384:576].set(v_bias.reshape(count_t, 192))
    params = pltpu.CompilerParams(dimension_semantics=("arbitrary",), vmem_limit_bytes=VMEM_LIMIT)

    query, key, value, out, attn = pl.pallas_call(
        partial(attend_kernel, windows=windows, padded=padded, keys=keys),
        grid=(count_t,),
        in_specs=[
            once((rows, width)),
            pl.BlockSpec((None, None, width, 384), lambda t: (t, 0, 0, 0)),
            pl.BlockSpec((None, None, width, 384), lambda t: (t, 1, 0, 0)),
            once((1, width)), once((1, width)),
            pl.BlockSpec((None, 1, 640), lambda t: (t, 0, 0)),
            once((2, 256, 384)), once((rows, 128)), once((padded, 128)),
        ],
        out_specs=[
            pl.BlockSpec((1, 3, rows, 128), lambda t: (t, 0, 0, 0)),
            pl.BlockSpec((1, 3, windows, keys, 128), lambda t: (t, 0, 0, 0, 0)),
            pl.BlockSpec((1, 3, windows, keys, 128), lambda t: (t, 0, 0, 0, 0)),
            pl.BlockSpec((1, rows, 256), lambda t: (t, 0, 0)),
            whole((rows, width)),
        ],
        out_shape=[
            jax.ShapeDtypeStruct((count_t, 3, rows, 128), BF),
            jax.ShapeDtypeStruct((count_t, 3, windows, keys, 128), BF),
            jax.ShapeDtypeStruct((count_t, 3, windows, keys, 128), BF),
            jax.ShapeDtypeStruct((count_t, rows, 256), BF),
            jax.ShapeDtypeStruct((rows, width), F32),
        ],
        scratch_shapes=[pltpu.VMEM((rows, width), BF), pltpu.VMEM((rows, 384), BF), pltpu.VMEM((rows, 256), BF)],
        compiler_params=params,
        name="attend",
    )(x, w_att, w_att, row(norm1_gain), row(norm1_bias), bias_att, spread_table, key_feat, amount)

    tiles = 2 * count_t
    result, gx1, grad_up, grad_down, gbias_up, small2 = pl.pallas_call(
        mlp_kernel,
        grid=(tiles,),
        in_specs=[
            once((rows, width)), once((rows, width)), once((rows, width)), once((rows, 128)),
            pl.BlockSpec((None, width, 384), lambda j: (j, 0, 0)),
            pl.BlockSpec((None, width, 384), lambda j: (j, 0, 0)),
            pl.BlockSpec((1, 1, 384), lambda j: (j, 0, 0)),
            once((1, width)), once((1, width)), once((1, width)), once((1, width)),
        ],
        out_specs=[
            whole((rows, width)), whole((rows, width)),
            pl.BlockSpec((1, width, 384), lambda j: (j, 0, 0)),
            pl.BlockSpec((1, width, 384), lambda j: (j, 0, 0)),
            pl.BlockSpec((1, 1, 384), lambda j: (j, 0, 0)),
            whole((8, width)),
        ],
        out_shape=[
            jax.ShapeDtypeStruct((rows, width), BF),
            jax.ShapeDtypeStruct((rows, width), F32),
            jax.ShapeDtypeStruct((tiles, width, 384), BF),
            jax.ShapeDtypeStruct((tiles, width, 384), BF),
            jax.ShapeDtypeStruct((tiles, 1, 384), F32),
            jax.ShapeDtypeStruct((8, width), F32),
        ],
        scratch_shapes=[
            pltpu.VMEM((rows, width), F32), pltpu.VMEM((rows, width), BF),
            pltpu.VMEM((width, rows), BF), pltpu.VMEM((width, rows), BF),
            pltpu.VMEM((rows, width), F32), pltpu.VMEM((rows, width), F32),
        ],
        compiler_params=params,
        name="mlp",
    )(
        x, attn, gy, live, w_up, w_down, fc1_bias.reshape(tiles, 1, 384),
        row(norm2_gain), row(norm2_bias), row(proj_bias), row(fc2_bias),
    )

    grad_x, grad_att, small1, gbias_att, grel = pl.pallas_call(
        partial(attend_back_kernel, windows=windows, padded=padded, keys=keys),
        grid=(count_t,),
        in_specs=[
            once((rows, width)), once((rows, width)),
            pl.BlockSpec((None, None, width, 384), lambda t: (t, 0, 0, 0)),
            pl.BlockSpec((None, None, width, 384), lambda t: (t, 1, 0, 0)),
            once((1, width)), once((1, width)), once((128, 128)), once((padded, 128)),
            pl.BlockSpec((1, 3, rows, 128), lambda t: (t, 0, 0, 0)),
            pl.BlockSpec((1, 3, windows, keys, 128), lambda t: (t, 0, 0, 0, 0)),
            pl.BlockSpec((1, 3, windows, keys, 128), lambda t: (t, 0, 0, 0, 0)),
            pl.BlockSpec((1, rows, 256), lambda t: (t, 0, 0)),
        ],
        out_specs=[
            whole((rows, width)),
            pl.BlockSpec((1, 2, width, 384), lambda t: (t, 0, 0, 0)),
            whole((8, width)),
            pl.BlockSpec((1, 1, 640), lambda t: (t, 0, 0)),
            whole((128, 128)),
        ],
        out_shape=[
            jax.ShapeDtypeStruct((rows, width), BF),
            jax.ShapeDtypeStruct((count_t, 2, width, 384), BF),
            jax.ShapeDtypeStruct((8, width), F32),
            jax.ShapeDtypeStruct((count_t, 1, 640), F32),
            jax.ShapeDtypeStruct((128, 128), F32),
        ],
        scratch_shapes=[
            pltpu.VMEM((width, rows), BF), pltpu.VMEM((width, rows), BF), pltpu.VMEM((rows, width), BF),
            pltpu.VMEM((rows, width), F32), pltpu.VMEM((rows, 256), BF),
            pltpu.VMEM((rows, 384), BF), pltpu.VMEM((rows, 256), BF), pltpu.VMEM((3, rows, 128), BF),
        ],
        compiler_params=params,
        name="attend_back",
    )(
        x, gx1, w_att, w_att, row(norm1_gain), row(norm1_bias), back_table, amount, query, key, value, out
    )

    grad_up = grad_up.reshape(count_t, 2, count_dp, strip, 384).transpose(2, 0, 1, 3, 4)
    grad_down = grad_down.reshape(count_t, 2, count_dp, strip, 384).transpose(2, 0, 1, 3, 4)
    grad_mlp = jnp.concatenate([grad_up, grad_down], 2).reshape(count_dp * count_t, 4, strip, 384)
    grad_att = grad_att.reshape(count_t, 2, count_dp, strip, 384).transpose(2, 0, 1, 3, 4)
    grad_att = grad_att.reshape(count_dp * count_t, 2, strip, 384)
    sum_mlp = lax.psum_scatter(grad_mlp, AXES, scatter_dimension=0, tiled=False).astype(F32)
    sum_att = lax.psum_scatter(grad_att, AXES, scatter_dimension=0, tiled=False).astype(F32)
    grad_rel = 8.0 * (grel[64:, :64])
    small = lax.psum((small1[:3], small2[:3], gbias_att, gbias_up, grad_rel), AXES)
    small1, small2, gbias_att, gbias_up, grad_rel = small
    head_q, head_k = sum_att[0, :, :192], sum_att[0, :, 192:]
    head_v, head_p = sum_att[1, :, :192], sum_att[1, :, 192:]
    return (
        cut_rows(result),
        cut_rows(grad_x),
        jnp.stack([head_q, head_k, head_v]),
        head_p.T,
        jnp.concatenate([sum_mlp[0], sum_mlp[1]], 1),
        jnp.concatenate([sum_mlp[2], sum_mlp[3]], 1).T,
        small1[1],
        small1[2],
        gbias_att[:, 0, :192].reshape(-1),
        gbias_att[:, 0, 384:576].reshape(-1),
        grad_rel[:span][::-1],
        grad_rel[32 : 32 + span][::-1],
        small1[0],
        small2[0],
        small2[1],
        gbias_up.reshape(-1),
        small2[2],
    )


def solution(mesh):
    return jax.shard_map(
        shards,
        mesh=mesh,
        in_specs=(
            P(AXES, None), P(AXES, None), P(), P("dp"),
            P(None, "dp", "tensor"), P("tensor", "dp"), P("dp", "tensor"), P("tensor", "dp"),
        )
        + (P(),) * 11,
        out_specs=(
            P(AXES, None), P(AXES, None),
            P(None, "dp", "tensor"), P("tensor", "dp"), P("dp", "tensor"), P("tensor", "dp"),
        )
        + (P(),) * 11,
        check_vma=False,
    )
```

time: 1470 us -> 562 us (0.38)
  local copies, waits for them, and re-layouts: 566 us -> 78.4 us
  matrix products: 235 us -> 0 us
  waiting for transfers between devices: 457 us -> 263 us
  Pallas kernels: 0 us -> 142 us
  other arithmetic: 85.9 us -> 19.5 us
  blocking collectives: 99.9 us -> 41.8 us
    add x52 -> x0, local copies, waits for them, and re-layouts: 383 us -> none  [the longest x48 381 us: scores_of(): base.reshape(blocks, heads, size, size, size, size) + bias_h[..., :, None]]
    dot_general x81 -> x0, matrix products: 229 us -> none  [the longest x6 48.7 us: against(): lax.dot_general(left, right, (((1,), (1,)), ((), ())), preferred_element_...]
    pallas_call x0 -> x3, Pallas kernels: none -> 142 us  [the longest x1 61.9 us: shards(): pl.pallas_call(partial(attend_back_kernel, windows=windows, padded=padded...]
    reduce_scatter x6 -> x2, waiting for transfers between devices: 282 us -> 183 us  [the longest x1 139 us: shards(): lax.psum_scatter(grad_mlp, AXES, scatter_dimension=0, tiled=False)]
    reshape x18 -> x11, local copies, waits for them, and re-layouts: 83 us -> 12.6 us  [the longest x1 5.14 us: shards(): lax.all_gather(shard[:2], AXES, axis=0, tiled=False)]
    all_gather x6 -> x2, waiting for transfers between devices: 144 us -> 79.3 us  [the longest x1 43.2 us: shards(): lax.all_gather(shard[2:], AXES, axis=0, tiled=False)]
    reduce_sum x17 -> x0, other arithmetic: 59 us -> none  [the longest x4 37.4 us: attend_back(): grad_w = jnp.sum(split, -2)]
    all_gather x2 -> x0, blocking collectives: 57.8 us -> none  [the longest x1 30 us: shards(): lax.all_gather(qkv_w, 'dp', axis=1, tiled=True)]
  transfers between devices with their start and end apart: 14 -> 4, of which waited for: 11 -> 4; matrix products, arithmetic and copies ran while one was open for 36% -> 11% of each run, Pallas kernels for 0% -> 6%
where the time goes in v1:
time: 562 us; the launch traced here: 558 us
  waiting for transfers between devices  263 us (47%)
  Pallas kernels  142 us (25%)
  local copies, waits for them, and re-layouts  78.4 us (14%)
  blocking collectives  41.8 us (7%)
  other arithmetic  19.5 us (3%)
  between operations  14.2 us (3%)
    reduce_scatter x1, waiting for transfers between devices, shards(): lax.psum_scatter(grad_mlp, AXES, scatter_dimension=0, tiled=False)  139 us
    pallas_call x1, Pallas kernels, shards(): pl.pallas_call(partial(attend_back_kernel, windows=windows, padded=padded...  61.9 us
    pallas_call x1, Pallas kernels, shards(): pl.pallas_call(mlp_kernel, grid=(tiles,), in_specs=[once((rows, width)),...  44.7 us
    reduce_scatter x1, waiting for transfers between devices, shards(): lax.psum_scatter(grad_att, AXES, scatter_dimension=0, tiled=False)  44.4 us
    all_gather x1, waiting for transfers between devices, shards(): lax.all_gather(shard[2:], AXES, axis=0, tiled=False)  43.2 us
    psum x1, blocking collectives, shards(): lax.psum((small1[:3], small2[:3], gbias_att, gbias_up, grad_rel), AXES)  41.8 us
    all_gather x1, waiting for transfers between devices, shards(): lax.all_gather(shard[:2], AXES, axis=0, tiled=False)  36.1 us
    pallas_call x1, Pallas kernels, shards(): pl.pallas_call(partial(attend_kernel, windows=windows, padded=padded, key...  35.1 us
  transfers between devices with their start and end apart: 4, of which 4 were waited for; matrix products, arithmetic and copies ran while one was open for 11% of the time, Pallas kernels for 6%

profile of v1, /device:TPU:1, one launch (start us, length us, event | category | flops | bytes accessed | tf_op | source)
XLA Modules:
  0.0 558.3 jit_solution(10035017267791039748)
XLA Ops:
  7.3 0.9 slice_bitcast_fusion.11
  10.0 1.0 slice_bitcast_fusion.6
  13.6 1.3 and_reduce_fusion
  16.6 2.1 scatter.46
  18.7 2.1 scatter.51
  24.1 1.0 copy.94
  30.2 1.4 reshape.508
  35.3 1.4 broadcast_select_fusion.1
  37.5 1.2 pad.62
  38.8 1.1 pad.64
  41.6 36.1 %all-gather.5.cloned.1.call-done = bf16[64,96,384]{2,1,0:T(8,128)(2,1)} async-done(((bf16[2,96,384]{2,1,0:T(8,128)(2,1)}), bf16[64,96,384]{2,1,0:T(8,128)(2,1)}) %all-gather.5.cloned.1.call-update) | async-done | bytes 4718608 | tf_op jit(solution)/shard_map/all_gather | solution.py:348
  77.7 5.1 copy.87
  82.9 35.1 %attend.1 = (bf16[4,3,832,128]{3,2,1,0:T(8,128)(2,1)}, bf16[4,3,4,256,128]{4,3,2,1,0:T(8,128)(2,1)}, bf16[4,3,4,256,128]{4,3,2,1,0:T(8,128)(2,1)}, bf16[4,832,256]{2,1,0:T(8,128)(2,1)}, f32[832,768]{1,0:T(8,128)}) custom-call(bf16[832,768]{1,0:T(8,128)(2,1)} %bitcast.98, bf16[4,2,768,384]{3,2,1,0:T(8,128)(2,1)} %bitcast.91, ...), custom_call_target="tpu_custom_call" | custom-call | tf_op jit(solution)/shard_map/attend/pallas_call | solution.py:360
  117.9 43.2 %all-gather.7.cloned.1.call-done = bf16[128,96,384]{2,1,0:T(8,128)(2,1)} async-done(((bf16[4,96,384]{2,1,0:T(8,128)(2,1)}), bf16[128,96,384]{2,1,0:T(8,128)(2,1)}) %all-gather.7.cloned.1.call-update) | async-done | bytes 9437200 | tf_op jit(solution)/shard_map/all_gather | solution.py:349
  161.1 8.9 %copy.95 = bf16[4,4,8,96,384]{4,3,2,1,0:T(8,128)(2,1)} copy(bf16[4,4,8,96,384]{4,3,0,1,2:T(8,128)(2,1)} %bitcast.103) | data formatting | bytes 18874368 | tf_op jit(solution)/shard_map/transpose | solution.py:351
  170.0 4.9 fusion.6
  174.9 2.7 copy.96
  177.6 2.6 copy.97
  180.2 0.9 broadcast_in_dim.83.live_ref
  181.2 44.7 %mlp.1 = (bf16[832,768]{1,0:T(8,128)(2,1)}, f32[832,768]{1,0:T(8,128)}, bf16[8,768,384]{2,1,0:T(8,128)(2,1)}, bf16[8,768,384]{2,1,0:T(8,128)(2,1)}, f32[8,1,384]{2,1,0:T(1,128)}, /*index=5*/f32[8,768]{1,0:T(8,128)}) custom-call(bf16[832,768]{1,0:T(8,128)(2,1)} %bitcast.99, f32[832,768]{1,0:T(8,128)} %get-tuple-element.177.attn_ref, ...), custom_call_target="tpu_custom_call" | custom-call | tf_op jit(solution)/shard_map/mlp/pallas_call | solution.py:391
  225.9 61.9 %attend_back.1 = (bf16[832,768]{1,0:T(8,128)(2,1)}, bf16[4,2,768,384]{3,2,1,0:T(8,128)(2,1)}, f32[8,768]{1,0:T(8,128)}, f32[4,1,640]{2,1,0:T(1,128)}, f32[128,128]{1,0:T(8,128)}) custom-call(bf16[832,768]{1,0:T(8,128)(2,1)} %bitcast.100, f32[832,768]{1,0:T(8,128)} %get-tuple-element.179.gx1_ref, bf16[4,2,768,384]{3,2,1,0:T(8,128)(2,1)} %bitcast.93, ...), custom_call_target="tpu_custom_call" | custom-call | tf_op jit(solution)/shard_map/attend_back/pallas_call | solution.py:428
  287.8 8.0 %copy.98 = bf16[8,4,2,96,384]{3,4,2,1,0:T(8,128)(2,1)} copy(bf16[8,4,2,96,384]{4,3,0,2,1:T(8,128)(2,1)} %bitcast.108) | data formatting | bytes 9437184 | tf_op jit(solution)/shard_map/transpose | solution.py:469
  295.9 7.8 %pad_maximum_fusion = bf16[8,4,4,96,384]{4,3,0,2,1:T(8,128)(2,1)} fusion(bf16[8,4,2,96,384]{4,3,0,2,1:T(8,128)(2,1)} %bitcast.107, bf16[8,4,2,96,384]{4,3,0,2,1:T(8,128)(2,1)} %bitcast.106), kind=kLoop, calls=%fused_computation.1 | loop fusion | flops 4718592 | bytes 18874368 | tf_op jit(solution)/shard_map/concatenate | solution.py:468
  303.8 9.4 %copy.99 = bf16[8,4,4,96,384]{4,3,2,1,0:T(8,128)(2,1)} copy(bf16[8,4,4,96,384]{4,3,0,2,1:T(8,128)(2,1)} %pad_maximum_fusion) | data formatting | bytes 18874368 | tf_op jit(solution)/shard_map/concatenate | solution.py:468
  314.1 41.8 %all-reduce.7 = (f32[3,768]{1,0:T(4,128)S(1)}, f32[4,1,640]{2,1,0:T(1,128)S(1)}, f32[64,64]{1,0:T(8,128)S(1)}, f32[3,768]{1,0:T(4,128)S(1)}, f32[3072]{0:T(1024)}) all-reduce(f32[3,768]{1,0:T(4,128)S(1)} %slice.386, f32[4,1,640]{2,1,0:T(1,128)S(1)} %copy-done.7, ...), channel_id=1, replica_groups=mesh['dp'=8,'tensor'=4] {'dp','tensor'}, use_global_device_ids=true, to_apply=%region_4.5 | all-reduce | flops 14336 | bytes 114688 | tf_op jit(solution)/shard_map/psum | solution.py:474
  358.5 1.4 slice.406
  359.8 1.2 reshape.520
  361.1 1.2 reshape.518
  363.5 44.4 %reduce-scatter.3.cloned.1.call-done = bf16[1,2,96,384]{2,3,1,0:T(8,128)(2,1)} async-done(((bf16[32,2,96,384]{2,3,1,0:T(8,128)(2,1)}), bf16[1,2,96,384]{2,3,1,0:T(8,128)(2,1)}) %reduce-scatter.3.cloned.1.call-update) | async-done | bytes 147472 | tf_op jit(solution)/shard_map/reduce_scatter | solution.py:472
  407.9 1.0 bitcast_convert_fusion
  410.5 138.7 %reduce-scatter.5.cloned.1.call-done = bf16[1,4,96,384]{3,2,1,0:T(8,128)(2,1)} async-done(((bf16[32,4,96,384]{3,2,1,0:T(8,128)(2,1)}), bf16[1,4,96,384]{3,2,1,0:T(8,128)(2,1)}) %reduce-scatter.5.cloned.1.call-update) | async-done | bytes 294928 | tf_op jit(solution)/shard_map/reduce_scatter | solution.py:471
  549.2 1.0 convert_element_type.39
  (112 shorter events, 28.4 us)
Async XLA Ops:
  7.2 27.4 %copy-start.17 = (s32[3]{0:T(128)S(1)}, s32[3]{0:T(128)}, u32[]{:S(2)}) copy-start(s32[3]{0:T(128)} %constant.335.clone.1) | copy-start | bytes 40
  7.2 21.6 %copy-start = (bf16[784,768]{1,0:T(8,128)(2,1)S(1)}, bf16[784,768]{1,0:T(8,128)(2,1)}, u32[]{:S(2)}) copy-start(bf16[784,768]{1,0:T(8,128)(2,1)} %param.46) | copy-start | bytes 3612676
  7.2 21.8 %copy-start.10 = (f32[768]{0:T(1024)S(1)}, f32[768]{0:T(1024)}, u32[]{:S(2)}) copy-start(f32[768]{0:T(1024)} %param.54) | copy-start | bytes 9220
  7.2 22.4 %copy-start.11 = (f32[768]{0:T(1024)S(1)}, f32[768]{0:T(1024)}, u32[]{:S(2)}) copy-start(f32[768]{0:T(1024)} %param.55) | copy-start | bytes 9220
  7.2 24.6 %copy-start.12 = (f32[768]{0:T(1024)S(1)}, f32[768]{0:T(1024)}, u32[]{:S(2)}) copy-start(f32[768]{0:T(1024)} %param.61) | copy-start | bytes 9220
  7.2 25.1 %copy-start.13 = (f32[768]{0:T(1024)S(1)}, f32[768]{0:T(1024)}, u32[]{:S(2)}) copy-start(f32[768]{0:T(1024)} %param.62) | copy-start | bytes 9220
  7.3 25.7 %copy-start.14 = (f32[768]{0:T(1024)S(1)}, f32[768]{0:T(1024)}, u32[]{:S(2)}) copy-start(f32[768]{0:T(1024)} %param.60) | copy-start | bytes 9220
  7.3 26.3 %copy-start.15 = (f32[768]{0:T(1024)S(1)}, f32[768]{0:T(1024)}, u32[]{:S(2)}) copy-start(f32[768]{0:T(1024)} %param.64) | copy-start | bytes 9220
  7.3 70.4 %all-gather.5.cloned.1.call-start = ((), (), s32[]{:S(2)}) async-start(), calls=%async_computation.4 | async-start | bytes 4866048 | tf_op jit(solution)/shard_map/all_gather | solution.py:348
  10.0 151.1 %all-gather.7.cloned.1.call-start = ((), (), s32[]{:S(2)}) async-start(), calls=%async_computation.5 | async-start | bytes 9732096 | tf_op jit(solution)/shard_map/all_gather | solution.py:349
  11.8 396.1 %reduce-scatter.3.cloned.1.call-start = ((), (), s32[]{:S(2)}) async-start(), calls=%async_computation.2 | async-start | bytes 6488064 | tf_op jit(solution)/shard_map/reduce_scatter | solution.py:472
  30.2 9.7 %copy-start.3 = (bf16[208,128]{1,0:T(8,128)(2,1)S(1)}, bf16[208,128]{1,0:T(8,128)(2,1)}, u32[]{:S(2)}) copy-start(bf16[208,128]{1,0:T(8,128)(2,1)} %constant.419) | copy-start | bytes 159748
  30.2 9.7 %copy-start.16 = (pred[128]{0:T(512)(128)(4,1)S(1)}, pred[128]{0:T(512)(128)(4,1)}, u32[]{:S(2)}) copy-start(pred[128]{0:T(512)(128)(4,1)} %constant.370) | copy-start | bytes 388
  34.6 48.3 %copy-start.2 = (bf16[128,128]{1,0:T(8,128)(2,1)}, bf16[128,128]{1,0:T(8,128)(2,1)S(1)}, u32[]{:S(2)}) copy-start(bf16[128,128]{1,0:T(8,128)(2,1)S(1)} %scatter.59.table_ref) | copy-start | bytes 98308
  37.5 45.4 %copy-start.4 = (f32[4,1,640]{2,1,0:T(1,128)}, f32[4,1,640]{2,1,0:T(1,128)S(1)}, u32[]{:S(2)}) copy-start(f32[4,1,640]{2,1,0:T(1,128)S(1)} %scatter.41.bias_ref) | copy-start | bytes 30724
  295.9 253.3 %reduce-scatter.5.cloned.1.call-start = ((), (), s32[]{:S(2)}) async-start(), calls=%async_computation.3 | async-start | bytes 9732096 | tf_op jit(solution)/shard_map/reduce_scatter | solution.py:471
  313.2 0.7 copy-start.9
  313.2 0.8 copy-start.8
  313.2 0.9 copy-start.5
  313.2 0.9 copy-start.6
  313.2 0.9 copy-start.7
  313.2 47.8 %copy-start.1 = (bf16[832,768]{1,0:T(8,128)(2,1)S(1)}, bf16[832,768]{1,0:T(8,128)(2,1)}, u32[]{:S(2)}) copy-start(bf16[832,768]{1,0:T(8,128)(2,1)} %get-tuple-element.178) | copy-start | bytes 3833860
Sparse Core Ops, SparseCore 0:
  11.6 66.1 all-gather.4
  81.2 79.8 all-gather.6
  296.0 111.9 reduce-scatter.2
  413.7 135.4 reduce-scatter.4

commit v2 on v1

v2 whole, which is shorter than its diff:
```python
from functools import partial

import jax
import jax.numpy as jnp
import numpy as np
from jax import lax
from jax.experimental import pallas as pl
from jax.experimental.pallas import tpu as pltpu
from jax.sharding import PartitionSpec as P

HD = 64
EPSILON = 1e-06
NEGATIVE = -1e30
F32, BF = jnp.float32, jnp.bfloat16
AXES = ("dp", "tensor")
VMEM_LIMIT = 60 * 1024 * 1024
MLP_PARTS = 1
MLP_BEGIN = (11,)
MLP_SLOTS = tuple(int(i * 2.8) for i in range(15))


def nn(left, right):
    return lax.dot_general(left, right, (((1,), (0,)), ((), ())), preferred_element_type=F32)


def nt(left, right):
    return lax.dot_general(left, right, (((1,), (1,)), ((), ())), preferred_element_type=F32)


def tn(left, right):
    return lax.dot_general(left, right, (((0,), (0,)), ((), ())), preferred_element_type=F32)


def normed_of(values):
    center = values - jnp.mean(values, -1, keepdims=True)
    inverse = lax.rsqrt(jnp.mean(center * center, -1, keepdims=True) + EPSILON)
    return center * inverse, inverse


def norm_back(grad, normed, inverse, gain):
    scaled = grad * gain
    inner = (
        scaled
        - jnp.mean(scaled, -1, keepdims=True)
        - normed * jnp.mean(scaled * normed, -1, keepdims=True)
    )
    return inverse * inner


def spread_rows(source_ref, target_ref, windows, padded, scale=None):
    length = source_ref.shape[0] // windows
    for w in range(windows):
        tail = w * padded + length // 16 * 16
        target_ref[tail : w * padded + padded, :] = jnp.zeros((w * padded + padded - tail, target_ref.shape[1]), target_ref.dtype)
        values = source_ref[w * length : w * length + length, :]
        if scale is not None:
            values = jnp.where(scale(w) > 0.5, values.astype(F32), 0.0).astype(values.dtype)
        target_ref[w * padded : w * padded + length, :] = values


def row(ref):
    return ref[...].reshape(1, -1)


def flat(values):
    return values.reshape(-1, values.shape[-1])


def lanes_of(shape):
    return lax.broadcasted_iota(jnp.int32, shape, 1)


def of_slot(values, slot):
    return jnp.sum(jnp.where(lanes_of(values.shape) == slot, values, 0.0), -1, keepdims=True)


def alive_of(slots_ref, slot):
    return of_slot(jnp.where(slots_ref[...] >= 0, 1.0, 0.0), slot)


def shift_lanes(values, amounts, left):
    for bit in (1, 2, 4, 8):
        moved = pltpu.roll(values, 128 - bit if left else bit, 1)
        values = jnp.where((amounts & bit) != 0, moved, values)
    return values


MESH = pl.DeviceIdType.MESH


class Place:
    def __init__(self, height):
        self.height = height
        self.dp, self.tensor = lax.axis_index("dp"), lax.axis_index("tensor")
        self.z, self.y = lax.div(self.dp, 2), lax.rem(self.dp, 2)
        self.x, self.c = lax.div(self.tensor, 2), lax.rem(self.tensor, 2)

    def plane(self, colour, a, b):
        return lax.rem(self.y + (1 - colour) * b + colour * a, 2), lax.rem(self.x + (1 - colour) * a + colour * b, 2)

    def shard(self, colour, a, b, z):
        y, x = self.plane(colour, a, b)
        return z * 2 + y, x * 2 + colour

    def near(self, k):
        upper = lax.div(self.z, self.height // 2)
        zz = self.z + upper * (self.height - 1 - 2 * self.z)
        q = (zz, 1 - zz, 2, 3)[k]
        return q + upper * (self.height - 1 - 2 * q)

    def peer(self, kind):
        if kind == "core":
            return self.dp, self.x * 2 + 1 - self.c
        if kind in ("z1", "z2", "z3"):
            return self.near(int(kind[1])) * 2 + self.y, self.tensor
        if kind == "up":
            return self.dp + 2, self.tensor
        if kind == "down":
            return self.dp - 2, self.tensor
        if kind == "y":
            return self.z * 2 + 1 - self.y, self.tensor
        if kind == "x":
            return self.dp, (1 - self.x) * 2 + self.c
        if kind == "pair":
            return (self.z + 1 - 2 * lax.rem(self.z, 2)) * 2 + self.y, self.tensor
        if kind == "half":
            return lax.rem(self.z + 2, 4) * 2 + self.y, self.tensor
        return self.shard(self.c, int(kind == "far"), int(kind == "near"), self.z)

    def has(self, kind):
        if kind == "up":
            return self.z < self.height - 1
        if kind == "down":
            return self.z > 0
        return None

    def greet(self):
        barrier = pltpu.get_barrier_semaphore()
        for kind in ("core", "near", "far", "z1", "z2", "z3"):
            pl.semaphore_signal(barrier, inc=1, device_id=self.peer(kind), device_id_type=MESH)
        pl.semaphore_wait(barrier, 6)


def under(condition, action):
    if condition is None:
        action()
    else:
        pl.when(condition)(action)


def both(one, two):
    return two if one is None else one if two is None else jnp.logical_and(one, two)


class Gather:
    SENDS = 36

    def __init__(self, at, own_ref, all_ref, send_sem, recv_sem, first=0, count=None):
        self.at, self.own_ref = at, own_ref
        self.all_ref = all_ref if count is None else all_ref.at[:, :, first : first + count]
        self.send_sem, self.recv_sem = send_sem, recv_sem
        z = [lambda k=k: self.step(("z", k)) for k in range(4)]
        near = [lambda k=k: self.step(("near", k)) for k in range(4)]
        far = [[lambda b=b, k=k: self.step(("far", b, k)) for k in range(4)] for b in range(2)]
        self.steps = [
            near[0], z[1], far[0][0], near[1], far[1][0], z[2], far[0][1],
            near[2], far[1][1], z[3], far[0][2], near[3], far[1][2], far[0][3], far[1][3],
        ]
        slot = 0
        self.slots = {}
        for key in [("z", k) for k in range(4)] + [("near", k) for k in range(4)] + [("far", b, k) for b in range(2) for k in range(4)]:
            self.slots[key] = slot
            slot += len(self.kinds(key))

    def kinds(self, key):
        return {"z": ("up", "down", "near", "far", "core"), "near": ("far", "core"), "far": ("core",)}[key[0]]

    def shard(self, key):
        at = self.at
        if key[0] == "z":
            return at.shard(at.c, 0, 0, at.near(key[1]))
        if key[0] == "near":
            return at.shard(at.c, 0, 1, at.near(key[1]))
        return at.shard(at.c, 1, key[1], at.near(key[2]))

    def copy(self, source, shard, kind, slot):
        dp, tensor = shard
        return pltpu.make_async_remote_copy(
            src_ref=source, dst_ref=self.all_ref.at[dp, tensor], send_sem=self.send_sem.at[slot],
            recv_sem=self.recv_sem.at[dp * 4 + tensor], device_id=self.at.peer(kind), device_id_type=MESH)

    def sends(self, key):
        shard = self.shard(key)
        source = self.own_ref if key == ("z", 0) else self.all_ref.at[shard[0], shard[1]]
        away = self.at.near(key[1]) - self.at.z if key[0] == "z" else 0
        sends = []
        for i, kind in enumerate(self.kinds(key)):
            condition = self.at.has(kind)
            if kind in ("up", "down"):
                condition = jnp.logical_and(condition, away <= 0 if kind == "up" else away >= 0)
            sends.append((condition, self.copy(source, shard, kind, self.slots[key] + i)))
        return sends

    def take(self, shard):
        self.copy(self.all_ref.at[shard[0], shard[1]], shard, "core", 0).wait_recv()

    def begin(self):
        for condition, copy in self.sends(("z", 0)):
            under(condition, copy.start)

    def step(self, key):
        self.take(self.shard(key))
        for condition, copy in self.sends(key):
            under(condition, copy.start)

    def arrive(self):
        at = self.at
        for a in range(2):
            for b in range(2):
                for k in range(4):
                    self.take(at.shard(1 - at.c, a, b, at.near(k)))

    def finish(self):
        for key in self.slots:
            for condition, copy in self.sends(key):
                under(condition, copy.wait_send)


def gather_scratch():
    return [pltpu.SemaphoreType.DMA((Gather.SENDS,)), pltpu.SemaphoreType.DMA((32,))]


class Scatter:
    def __init__(self, all_ref, own_ref, held, core_in, far_in, near_in, up_in, down_in, sems, height=4):
        self.all_ref, self.own_ref, self.held, self.core_in = all_ref, own_ref, held, core_in
        self.far_in, self.near_in, self.up_in, self.down_in, self.sems = far_in, near_in, up_in, down_in, sems
        self.at = Place(height)
        core = {(a, b): (lambda a=a, b=b: self.from_core(a, b)) for a in range(2) for b in range(2)}
        far = [[lambda b=b, k=k: self.from_far(b, k) for k in range(4)] for b in range(2)]
        near = [lambda k=k: self.from_near(k) for k in range(4)]
        line = [lambda k=k: self.from_line(k) for k in range(4)]
        self.steps = [
            [self.begin], [core[1, 1], core[1, 0]], [core[0, 1], core[0, 0]], [far[1][3]], [far[1][2]],
            [far[1][1], near[3]], [far[1][0], near[2]], [far[0][3], near[1]], [far[0][2], line[3]], [near[0], far[0][1]],
            [line[2]], [far[0][0]], [line[1]], [], [],
        ]
        self.last = line[0]

    def remote(self, source, target, name, index, kind):
        send, recv = self.sems[name]
        return pltpu.make_async_remote_copy(
            src_ref=source, dst_ref=target, send_sem=send.at[index], recv_sem=recv.at[index],
            device_id=self.at.peer(kind), device_id_type=MESH)

    def core_copy(self, a, b):
        at = self.at
        y, x = at.plane(1 - at.c, a, b)
        source = self.all_ref.at[:, y, x * 2 + 1 - at.c]
        return self.remote(source, self.core_in.at[a, b], "core", a * 2 + b, "core")

    def local_copy(self, a, b):
        at = self.at
        y, x = at.plane(at.c, a, b)
        return pltpu.make_async_copy(self.all_ref.at[:, y, x * 2 + at.c], self.held.at[a, b], self.sems["local"].at[a * 2 + b])

    def far_copy(self, b, z):
        return self.remote(self.held.at[1, b, z], self.far_in.at[b, z], "far", b * 4 + z, "far")

    def near_copy(self, z):
        return self.remote(self.held.at[0, 1, z], self.near_in.at[z], "near", z, "near")

    def down_copy(self, z):
        return self.remote(self.held.at[0, 0, z], self.down_in.at[z], "down", z, "down")

    def up_copy(self, z):
        return self.remote(self.held.at[0, 0, z], self.up_in.at[z], "up", z, "up")

    def begin(self):
        self.at.greet()
        for a in (1, 0):
            for b in (1, 0):
                self.core_copy(a, b).start()
                self.local_copy(a, b).start()

    def from_core(self, a, b):
        self.local_copy(a, b).wait()
        self.core_copy(a, b).wait_recv()
        for z in range(4):
            self.held[a, b, z] = self.held[a, b, z] + self.core_in[a, b, z]
        if a == 1:
            for k in (3, 2, 1, 0):
                self.far_copy(b, self.at.near(k)).start()

    def from_far(self, b, k):
        z = self.at.near(k)
        self.far_copy(b, z).wait_recv()
        self.held[0, b, z] = self.held[0, b, z] + self.far_in[b, z]
        if b == 1:
            self.near_copy(z).start()

    def from_near(self, k):
        z = self.at.near(k)
        self.near_copy(z).wait_recv()
        self.held[0, 0, z] = self.held[0, 0, z] + self.near_in[z]

    def from_line(self, k):
        at = self.at
        if k > 0:
            z = at.near(k)

            def downward():
                def add():
                    self.down_copy(z).wait_recv()
                    self.held[0, 0, z] = self.held[0, 0, z] + self.down_in[z]

                under(at.has("up"), add)
                self.down_copy(z).start()

            def upward():
                def add():
                    self.up_copy(z).wait_recv()
                    self.held[0, 0, z] = self.held[0, 0, z] + self.up_in[z]

                under(at.has("down"), add)
                self.up_copy(z).start()

            pl.when(z < at.z)(downward)
            pl.when(z > at.z)(upward)
            return
        self.own_ref[...] = self.held[0, 0, at.z].astype(F32)

        def add_down():
            self.down_copy(at.z).wait_recv()
            self.own_ref[...] += self.down_in[at.z].astype(F32)

        def add_up():
            self.up_copy(at.z).wait_recv()
            self.own_ref[...] += self.up_in[at.z].astype(F32)

        under(at.has("up"), add_down)
        under(at.has("down"), add_up)

    def finish(self):
        at = self.at
        self.last()
        for a in range(2):
            for b in range(2):
                self.core_copy(a, b).wait_send()
        for b in range(2):
            for z in range(4):
                self.far_copy(b, z).wait_send()
        for z in range(4):
            self.near_copy(z).wait_send()
            pl.when(z < at.z)(lambda: self.down_copy(z).wait_send())
            pl.when(z > at.z)(lambda: self.up_copy(z).wait_send())


def scatter_scratch(pieces, strip, columns):
    block = (pieces, strip, columns)
    shapes = [(2, 2, 4), (2, 2, 4), (2, 4), (4,), (4,), (4,)]
    sems = [4, 4, 8, 8, 4, 4, 4, 4, 4, 4, 4]
    return [pltpu.VMEM(lead + block, BF) for lead in shapes] + [pltpu.SemaphoreType.DMA((n,)) for n in sems]


SCATTER_REFS = 17


def make_scatter(all_ref, own_ref, refs):
    held, core_in, far_in, near_in, up_in, down_in = refs[:6]
    core_s, core_r, far_s, far_r, near_s, near_r, up_s, up_r, down_s, down_r, local = refs[6:]
    sems = {
        "core": (core_s, core_r), "far": (far_s, far_r), "near": (near_s, near_r),
        "up": (up_s, up_r), "down": (down_s, down_r), "local": local,
    }
    return Scatter(all_ref, own_ref, held, core_in, far_in, near_in, up_in, down_in, sems)


def packed(refs):
    small1_ref, small2_ref, gbias_att_ref, gbias_up_ref = refs
    places = []
    for ref, rows in ((small1_ref, range(3)), (small2_ref, range(3))):
        places += [(ref, (row, lane)) for row in rows for lane in range(0, ref.shape[1], 128)]
    for ref in (gbias_att_ref, gbias_up_ref):
        places += [(ref, (row, 0, lane)) for row in range(ref.shape[0]) for lane in range(0, ref.shape[2], 128)]
    return places


def reduce_kernel(
    all_ref, small1_ref, small2_ref, gbias_att_ref, gbias_up_ref, grel_ref,
    own_ref, total_ref, small_ref, small_in, small_send, small_recv, *refs,
):
    scatter = make_scatter(all_ref, own_ref, refs)
    at = scatter.at
    rounds = ("core", "y", "x", "pair", "half")

    def exchange(index):
        return pltpu.make_async_remote_copy(
            src_ref=small_ref if index == 0 else small_in.at[5 + index], dst_ref=small_in.at[index],
            send_sem=small_send.at[index], recv_sem=small_recv.at[index],
            device_id=at.peer(rounds[index]), device_id_type=MESH)

    def fold(index):
        exchange(index).wait_recv()
        own = small_ref[...] if index == 0 else small_in[5 + index]
        if index < 4:
            small_in[6 + index] = own + small_in[index]
            exchange(index + 1).start()
        else:
            total_ref[...] = own + small_in[index]

    scatter.begin()
    for row, (ref, index) in enumerate(packed((small1_ref, small2_ref, gbias_att_ref, gbias_up_ref))):
        if len(index) == 2:
            small_ref[row : row + 1, :] = ref[index[0] : index[0] + 1, index[1] : index[1] + 128]
        else:
            small_ref[row : row + 1, :] = ref[index[0], 0:1, index[2] : index[2] + 128]
    small_ref[small_ref.shape[0] - 64 :, :] = grel_ref[64:, :]
    exchange(0).start()
    for step in scatter.steps[1]:
        step()
    fold(0)
    for step in scatter.steps[2]:
        step()
    fold(1)
    for number, steps in enumerate(scatter.steps[3:]):
        for step in steps:
            step()
        if number in (0, 2, 4):
            fold(2 + number // 2)
    scatter.finish()
    for index in range(5):
        exchange(index).wait_send()


def attend_kernel(*refs, windows, padded, keys, size, linked):
    step = pl.program_id(0)
    duties = {}
    refs = list(refs)
    if linked:
        own_ref, att_ref, mlp_ref, w_ref, keep_sem = refs[10], refs[17], refs[18], refs[25], refs[-1]
        at = Place(4)
        att = Gather(at, own_ref.at[:2], w_ref, *refs[26:28])
        share = 4 // MLP_PARTS
        mlp = [
            Gather(at, own_ref.at[2 + i * share : 2 + i * share + share], mlp_ref, *refs[28 + 2 * i : 30 + 2 * i], i * share, share)
            for i in range(MLP_PARTS)
        ]
        todo = [act for acts in zip(*[part.steps for part in mlp]) for act in acts]
        mine = pltpu.make_async_copy(own_ref.at[2:], mlp_ref.at[at.dp, at.tensor], keep_sem.at[0])
        keep = pltpu.make_async_copy(w_ref, att_ref, keep_sem.at[1])
        refs = refs[:1] + [w_ref] + refs[1:10] + refs[11:17] + refs[19:25]

        @pl.when(step == 0)
        def _():
            at.greet()
            att.begin()
            w_ref[at.dp, at.tensor] = own_ref[:2]
            mine.start()

        duties = {slot: [todo[i] for i in range(len(todo)) if MLP_SLOTS[i] == slot] for slot in MLP_SLOTS}
    (
        raw_ref, w_ref, gain_ref, shift_ref, query_bias_ref, value_bias_ref, rel_ref, slots_ref, pad_ref, feat_ref, amount_ref,
        query_ref, key_ref, value_ref, out_ref, acc_ref, x_ref,
        h1_ref, qk_ref, vv_ref, table_ref, key_feat_ref, bias_ref,
    ) = refs

    @pl.when(step == 0)
    def _():
        length = pad_ref.shape[0]
        spread_rows(raw_ref, x_ref, windows, padded)
        normed, _ = normed_of(x_ref[...].astype(F32))
        h1_ref[...] = (normed * row(gain_ref) + row(shift_ref)).astype(BF)
        acc_ref[...] = jnp.zeros_like(acc_ref)

        span = 2 * size - 1
        place = lax.broadcasted_iota(jnp.int32, (64, 128), 0)
        lane = lanes_of((64, 128))
        wanted = jnp.where(place < span, 64 + span - 1 - place, jnp.where(place < 2 * span, 96 + 2 * span - 1 - place, -1))
        chosen = jnp.where(lane == wanted, 1.0, 0.0).astype(BF)
        rel = rel_ref[...]
        high = rel.astype(BF)
        rest = (rel - high.astype(F32)).astype(BF)
        table_ref[...] = jnp.zeros_like(table_ref)
        for number, piece in enumerate((high, rest)):
            turned = tn(piece, chosen)[:64].astype(BF)
            for head in range(3):
                table_ref[number, head * 64 : head * 64 + 64, head * 128 : head * 128 + 128] = turned

        part = lax.axis_index("tensor")
        count = pad_ref.shape[1]
        picked = jnp.where(lax.broadcasted_iota(jnp.int32, (count, 128), 0) == slots_ref[...], 1.0, 0.0).astype(BF)
        usable = nn(pad_ref[...].astype(F32).astype(BF), picked)
        for w in range(windows):
            mask = jnp.where(of_slot(usable, part * windows + w) > 0.5, 0.0, NEGATIVE)
            start = w * padded
            key_feat_ref[start : start + padded, :] = feat_ref[...]
            key_feat_ref[start : start + length, :] = jnp.where(
                lanes_of((length, 128)) == 79, mask, feat_ref[:length, :].astype(F32)).astype(BF)
        bias_ref[...] = jnp.zeros_like(bias_ref)
        for t in range(bias_ref.shape[0]):
            bias_ref[t, 0:1, 0:192] = row(query_bias_ref)[:, t * 192 : t * 192 + 192]
            bias_ref[t, 0:1, 384:576] = row(value_bias_ref)[:, t * 192 : t * 192 + 192]

        if linked:
            for number, act in enumerate(att.steps):
                act()
                if number in MLP_BEGIN:
                    mlp[MLP_BEGIN.index(number)].begin()
            att.arrive()
            keep.start()

    h1 = h1_ref[...]
    chunk = step if linked else 0
    wa, wb = flat(w_ref[:, chunk, 0]), flat(w_ref[:, chunk, 1])
    qk_ref[...] = (nn(h1, wa) + bias_ref[step, 0:1, :384]).astype(BF)
    vv_ref[...] = (nn(h1, wb[:, :256]) + bias_ref[step, 0:1, 384:640]).astype(BF)
    lane = lanes_of((padded, 128))
    low = lane < 64
    field = lane & 31
    amounts = amount_ref[...]
    pad_lane = lanes_of((keys - padded, 128))
    pad_key = jnp.where(pad_lane == 79, NEGATIVE, 0.0).astype(BF)

    def window(w, carry):
        rows = pl.ds(pl.multiple_of(w * padded, 16), padded)
        qk = qk_ref[rows, :]
        vv = vv_ref[rows, :]
        spread = nn(qk[:, :256], table_ref[0]) + nn(qk[:, :256], table_ref[1])
        wide = qk.astype(F32)
        wide_v = vv.astype(F32)
        parts = [wide[:, :128], wide[:, 128:256], wide[:, 256:384]]
        turned = [pltpu.roll(part, 64, 1) for part in parts]
        queries = [parts[0], turned[0], parts[1]]
        keys_low = [turned[1], parts[2], turned[2]]
        values = [wide_v[:, :128], pltpu.roll(wide_v[:, :128], 64, 1), wide_v[:, 128:256]]
        key_feat = key_feat_ref[rows, :].astype(F32)
        ones = jnp.where((lane == 64) | (lane == 65), 1.0, 0.0)
        outs = []
        for head in range(3):
            for slot in duties:
                if slot % 3 == head:
                    for act in duties[slot]:
                        pl.when(step * windows + w == slot // 3)(act)
            moved = shift_lanes(spread[:, head * 128 : head * 128 + 128], amounts, True)
            high = moved.astype(BF).astype(F32)
            rest = pltpu.roll(moved - high, 16, 1)
            feat = jnp.where(field < 16, high, rest)
            feat = jnp.where(field < 14, feat, jnp.where((field >= 16) & (field < 30), feat, 0.0))
            feat = jnp.where(lane == 79, 1.0, feat)
            query = jnp.where(low, queries[head] * 0.125, feat)
            key_ref[0, head, w, :padded, :] = jnp.where(low, keys_low[head], key_feat).astype(BF)
            key_ref[0, head, w, padded:, :] = pad_key
            value_ref[0, head, w, :padded, :] = jnp.where(low, values[head], ones).astype(BF)
            value_ref[0, head, w, padded:, :] = jnp.zeros((keys - padded, 128), BF)
            scores = nt(query.astype(BF), key_ref[0, head, w])
            top = jnp.max(scores, -1, keepdims=True)
            expo = jnp.exp(scores - top).astype(BF)
            mixed = nn(expo, value_ref[0, head, w])
            total = mixed[:, 64:65]
            outs.append(mixed / total)
            logsum = -(top + jnp.log(total))
            first = logsum.astype(BF).astype(F32)
            second = (logsum - first).astype(BF).astype(F32)
            third = logsum - first - second
            query = jnp.where(lane == 78, first, query)
            query = jnp.where(lane == 94, second, query)
            query = jnp.where(lane == 95, third, query)
            query_ref[0, head, rows, :] = query.astype(BF)
        out_ref[0, rows, :128] = jnp.where(low, 0.0, pltpu.roll(outs[0], 64, 1)).astype(BF)
        out_ref[0, rows, 128:] = jnp.where(low, outs[1], pltpu.roll(outs[2], 64, 1)).astype(BF)
        return carry

    lax.fori_loop(0, windows, window, 0)
    acc_ref[...] += nt(out_ref[0], flat(w_ref[:, chunk, 1])[:, 128:])
    if linked:

        @pl.when(step == pl.num_programs(0) - 1)
        def _():
            for part in mlp:
                part.arrive()
            mine.wait()
            keep.wait()
            for part in [att] + mlp:
                part.finish()


def mlp_kernel(
    x_ref, attn_ref, cotangent_ref, slots_ref, w_ref, bias_proj_ref, gain_ref, shift_ref, bias_down_ref, bias_up_ref,
    result_ref, gx1_ref, grad_ref, gbias_up_ref, small_ref,
    x1_ref, h2_ref, h2t_ref, gyt_ref, y_ref, dh_ref, gy_ref, bias_ref,
    *, windows, padded,
):
    first = lax.axis_index("tensor") * windows
    columns = w_ref.shape[5]
    step = pl.program_id(0)
    last = pl.num_programs(0) - 1

    @pl.when(step == 0)
    def _():
        spread_rows(cotangent_ref, gy_ref, windows, padded, lambda w: alive_of(slots_ref, first + w))
        x1 = x_ref[...].astype(F32) + (attn_ref[...] + row(bias_proj_ref))
        x1_ref[...] = x1
        normed, _ = normed_of(x1)
        h2 = (normed * row(gain_ref) + row(shift_ref)).astype(BF)
        for tile in range(bias_ref.shape[0]):
            bias_ref[tile] = row(bias_up_ref)[:, tile * columns : tile * columns + columns]
        h2_ref[...] = h2
        h2t_ref[...] = h2.T
        gyt_ref[...] = gy_ref[...].T
        y_ref[...] = jnp.zeros_like(y_ref)
        dh_ref[...] = jnp.zeros_like(dh_ref)

    up, down = flat(w_ref[:, 0, 0, 0]), flat(w_ref[:, 0, 1, 0])
    strips = (grad_ref.shape[0], grad_ref.shape[4], up.shape[1])
    upper = nn(h2_ref[...], up) + bias_ref[step]
    half = 0.5 * (1.0 + lax.erf(upper * np.float32(np.sqrt(0.5))))
    slope = half + upper * (np.float32(1.0 / np.sqrt(2 * np.pi)) * jnp.exp(-0.5 * upper * upper))
    active = (upper * half).astype(BF)
    grad_upper = (nn(gy_ref[...], down) * slope).astype(BF)
    y_ref[...] += nt(active, down)
    dh_ref[...] += nt(grad_upper, up)
    grad_ref[:, 0, 1, 0] = nn(gyt_ref[...], active).astype(BF).reshape(strips)
    grad_ref[:, 0, 0, 0] = nn(h2t_ref[...], grad_upper).astype(BF).reshape(strips)
    gbias_up_ref[0] = jnp.sum(grad_upper.astype(F32), 0, keepdims=True)

    @pl.when(step == last)
    def _():
        x1 = x1_ref[...]
        result = x1 + (y_ref[...] + row(bias_down_ref))
        length = result_ref.shape[0] // windows
        for w in range(windows):
            part = alive_of(slots_ref, first + w) * result[w * padded : w * padded + length]
            result_ref[w * length : w * length + length, :] = part.astype(BF)
        normed, inverse = normed_of(x1)
        gy = gy_ref[...].astype(F32)
        dh = dh_ref[...]
        gx1_ref[...] = gy + norm_back(dh, normed, inverse, row(gain_ref))
        small_ref[0:1, :] = jnp.sum(dh * normed, 0, keepdims=True)
        small_ref[1:2, :] = jnp.sum(dh, 0, keepdims=True)
        small_ref[2:3, :] = jnp.sum(gy, 0, keepdims=True)
        small_ref[3:8, :] = jnp.zeros_like(small_ref[3:8, :])


def attend_back_kernel(*refs, windows, padded, keys, size, linked):
    step = pl.program_id(0)
    last = pl.num_programs(0) - 1
    scatter = None
    if linked:
        scatter = make_scatter(refs[11], refs[17], refs[27:])
        refs = refs[:11] + refs[12:17] + refs[18:27]
        pl.when(step == 0)(scatter.begin)
    (
        x_ref, gx1_ref, w_ref, gain_ref, shift_ref, rel_ref, amount_ref,
        query_ref, key_ref, value_ref, out_ref,
        grad_x_ref, grad_ref, small_ref, gbias_ref, grel_ref,
        h1t_ref, gbt_ref, gb_ref, dh_ref, do_ref, gqk_ref, gv_ref, spread_ref, table_ref,
    ) = refs

    @pl.when(step == 0)
    def _():
        normed, _ = normed_of(x_ref[...].astype(F32))
        h1t_ref[...] = (normed * row(gain_ref) + row(shift_ref)).astype(BF).T
        span = 2 * size - 1
        place = lax.broadcasted_iota(jnp.int32, (64, 128), 0)
        wanted = jnp.where(place < span, span - 1 - place, jnp.where(place < 2 * span, 32 + 2 * span - 1 - place, -1))
        chosen = jnp.where((lanes_of((64, 128)) & 63) == wanted, 1.0, 0.0).astype(BF)
        table_ref[...] = tn(chosen, rel_ref[...].astype(BF)).astype(BF)
        gb = gx1_ref[...].astype(BF)
        gb_ref[...] = gb
        gbt_ref[...] = gb.T
        dh_ref[...] = jnp.zeros_like(dh_ref)
        grel_ref[...] = jnp.zeros_like(grel_ref)
        small_ref[0:1, :] = jnp.sum(gb.astype(F32), 0, keepdims=True)

    do_ref[...] = nn(gb_ref[...], flat(w_ref[:, 0, 1])[:, 128:]).astype(BF)
    lane = lanes_of((padded, 128))
    low = lane < 64
    field = lane & 31
    amounts = amount_ref[...]
    kept = (lane >= 64) & (field < 14)

    def window(w, carry):
        if linked:
            for number in range(1, len(scatter.steps)):
                for action in scatter.steps[number]:
                    pl.when(step * windows + w == number)(action)
        rows = pl.ds(pl.multiple_of(w * padded, 16), padded)
        do = do_ref[rows, :].astype(F32)
        out = out_ref[0, rows, :].astype(F32)
        product = do * out
        grads = [pltpu.roll(do[:, :128], 64, 1), do[:, 128:], pltpu.roll(do[:, 128:], 64, 1)]
        sums = [
            jnp.sum(jnp.where(low, 0.0, product[:, :128]), -1, keepdims=True),
            jnp.sum(jnp.where(low, product[:, 128:], 0.0), -1, keepdims=True),
            jnp.sum(jnp.where(low, 0.0, product[:, 128:]), -1, keepdims=True),
        ]
        gq, gk, gv = [], [], []
        for head in range(3):
            delta = -sums[head]
            first = delta.astype(BF).astype(F32)
            grad_out = jnp.where(low, grads[head], jnp.where(lane == 64, first, jnp.where(lane == 65, delta - first, 0.0))).astype(BF)
            query, key, value = query_ref[0, head, rows, :], key_ref[0, head, w], value_ref[0, head, w]
            prob = jnp.exp(nt(query, key))
            grad_scores = (prob * nt(grad_out, value)).astype(BF)
            gv.append(tn(prob.astype(BF), grad_out)[:padded])
            gk.append(tn(grad_scores, query)[:padded])
            both = nn(grad_scores, key)
            back = shift_lanes(jnp.where(kept, both, 0.0), amounts, False)
            high = back.astype(BF).astype(F32)
            pack = jnp.where(low, pltpu.roll(back - high, 64, 1), high).astype(BF)
            spread_ref[head, rows, :] = pack
            gq.append(both * 0.125 + nn(pack, table_ref[...]))
        gqk_ref[rows, :128] = jnp.where(low, gq[0], pltpu.roll(gq[1], 64, 1)).astype(BF)
        gqk_ref[rows, 128:256] = jnp.where(low, gq[2], pltpu.roll(gk[0], 64, 1)).astype(BF)
        gqk_ref[rows, 256:] = jnp.where(low, gk[1], pltpu.roll(gk[2], 64, 1)).astype(BF)
        gv_ref[rows, :128] = jnp.where(low, gv[0], pltpu.roll(gv[1], 64, 1)).astype(BF)
        gv_ref[rows, 128:] = jnp.where(low, gv[2], 0.0).astype(BF)
        return carry

    lax.fori_loop(0, windows, window, 0)
    for head in range(3):
        grel_ref[...] += tn(spread_ref[head], query_ref[0, head])
    gqk, gv = gqk_ref[...], gv_ref[...]
    gbias_ref[0, :, :384] = jnp.sum(gqk.astype(F32), 0, keepdims=True)
    gbias_ref[0, :, 384:] = jnp.sum(gv.astype(F32), 0, keepdims=True)
    dh_ref[...] += nt(gqk, flat(w_ref[:, 0, 0])) + nt(gv, flat(w_ref[:, 0, 1])[:, :256])
    h1t = h1t_ref[...]
    strips = (grad_ref.shape[0], grad_ref.shape[3], -1)
    grad_ref[:, 0, 0] = nn(h1t, gqk).astype(BF).reshape(strips)
    one, two = nn(h1t, gv), nn(gbt_ref[...], out_ref[0])
    grad_ref[:, 0, 1, :, :128] = one[:, :128].astype(BF).reshape(strips)
    grad_ref[:, 0, 1, :, 128:256] = (one[:, 128:] + two[:, :128]).astype(BF).reshape(strips)
    grad_ref[:, 0, 1, :, 256:] = two[:, 128:].astype(BF).reshape(strips)

    @pl.when(step == last)
    def _():
        normed, inverse = normed_of(x_ref[...].astype(F32))
        dh = dh_ref[...]
        grad_x = (gx1_ref[...] + norm_back(dh, normed, inverse, row(gain_ref))).astype(BF)
        length = grad_x_ref.shape[0] // windows
        for w in range(windows):
            grad_x_ref[w * length : w * length + length, :] = grad_x[w * padded : w * padded + length]
        small_ref[1:2, :] = jnp.sum(dh * normed, 0, keepdims=True)
        small_ref[2:3, :] = jnp.sum(dh, 0, keepdims=True)
        small_ref[3:8, :] = jnp.zeros_like(small_ref[3:8, :])
        if linked:
            scatter.finish()


def unpack_kernel(
    total_ref, att_ref, mlp_ref,
    qkv_ref, proj_ref, up_ref, down_ref, gain1_ref, shift1_ref, q_ref, v_ref, rel_h_ref, rel_w_ref,
    proj_bias_ref, gain2_ref, shift2_ref, up_bias_ref, down_bias_ref,
    *, span,
):
    qkv_ref[0] = att_ref[0, :, :192]
    qkv_ref[1] = att_ref[0, :, 192:]
    qkv_ref[2] = att_ref[1, :, :192]
    proj_ref[...] = att_ref[1, :, 192:].T
    up_ref[:, :384] = mlp_ref[0]
    up_ref[:, 384:] = mlp_ref[1]
    down_ref[:, :384] = mlp_ref[2]
    down_ref[:, 384:] = mlp_ref[3]
    for first, ref in ((0, proj_bias_ref), (6, gain1_ref), (12, shift1_ref), (18, gain2_ref), (24, shift2_ref), (30, down_bias_ref), (56, up_bias_ref)):
        for lane in range(0, ref.shape[0], 128):
            ref[pl.ds(lane, 128)] = total_ref[first + lane // 128]
    for start, ref in ((36, q_ref), (39, v_ref)):
        pieces = []
        for t in range(ref.shape[0] // 192):
            first = start + 5 * t
            pieces.append((total_ref[first : first + 1, :], total_ref[first + 1 : first + 2, :]))
        for pair in range(len(pieces) // 2):
            one, two = pieces[2 * pair], pieces[2 * pair + 1]
            low = lanes_of((1, 128)) < 64
            turned = [pltpu.roll(jnp.broadcast_to(v, (8, 128)), 64, 1)[:1] for v in two]
            parts = [one[0], jnp.where(low, one[1], turned[0]), jnp.where(low, turned[0], turned[1])]
            for i, values in enumerate(parts):
                ref[pl.ds(pair * 384 + i * 128, 128)] = values[0]
    rel = total_ref[total_ref.shape[0] - 64 :, :]
    high = rel.astype(BF)
    middle = (rel - high.astype(F32)).astype(BF)
    rest = (rel - high.astype(F32) - middle.astype(F32)).astype(BF)
    for ref, first in ((rel_h_ref, 0), (rel_w_ref, 32)):
        place = lax.broadcasted_iota(jnp.int32, (32, 64), 0)
        chosen = jnp.where(lanes_of((32, 64)) == first + span - 1 - place, 1.0, 0.0).astype(BF)
        values = nn(chosen, high) + nn(chosen, middle) + nn(chosen, rest)
        ref[...] = 8.0 * values[:span, :64]


def whole(shape):
    return pl.BlockSpec(shape, lambda *index: (0,) * len(shape))


def once(shape):
    return pl.BlockSpec(shape, lambda *index: (0,) * len(shape), pipeline_mode=pl.Buffered(1))


def shards(
    block_input, cotangent, pad_mask, slot_window, qkv_w, proj_w, fc1_w, fc2_w,
    norm1_gain, norm1_bias, q_bias, v_bias, rel_h, rel_w, proj_bias,
    norm2_gain, norm2_bias, fc1_bias, fc2_bias,
):
    part = lax.axis_index("tensor")
    count_dp, count_t = lax.axis_size("dp"), lax.axis_size("tensor")
    length = pad_mask.shape[1]
    local_rows, width = block_input.shape
    windows = local_rows // length
    size = rel_h.shape[0] // 2 + 1
    padded = -(-length // 16) * 16
    keys = -(-length // 128) * 128
    rows = windows * padded
    strip = width // count_dp

    slots = jnp.pad(slot_window, (0, 128 - slot_window.shape[0]), constant_values=-1).reshape(1, 128)
    rel = jnp.pad(jnp.concatenate([rel_h, rel_w]), ((0, 64 - 2 * rel_h.shape[0]), (0, 64)))

    place = np.arange(padded)
    row_of, col_of = place // size, place % size
    inside = place < length
    amount = np.zeros((padded, 128), np.int32)
    amount[:, :] = np.where(
        (np.arange(128) % 64 < 32)[None, :], (size - 1 - row_of)[:, None], (size - 1 - col_of)[:, None]
    ) * inside[:, None]
    amount = jnp.asarray(amount)
    feat = np.zeros((padded, 128), np.float32)
    for a in range(size):
        for base, pos in ((64, row_of), (96, col_of)):
            feat[:, base + a] = (pos == a) & inside
            feat[:, base + 16 + a] = (pos == a) & inside
    feat[:, [78, 94, 95]] = 1.0
    feat[:, 79] = np.where(inside, 0.0, NEGATIVE)
    feat = jnp.asarray(feat.astype(BF))
    span = rel_h.shape[0]

    q_w, k_w, v_w = qkv_w[0], qkv_w[1], qkv_w[2]
    shard = jnp.stack(
        [
            jnp.concatenate([q_w, k_w], 1),
            jnp.concatenate([v_w, proj_w.T], 1),
            fc1_w[:, :384],
            fc1_w[:, 384:],
            fc2_w.T[:, :384],
            fc2_w.T[:, 384:],
        ]
    )
    linked = count_dp == 8 and count_t == 4 and strip % 16 == 0 and windows == 4
    any_spec, vmem_spec = pl.BlockSpec(memory_space=pl.ANY), pl.BlockSpec(memory_space=pltpu.VMEM)
    blocks, depth = (count_dp, strip) if linked else (1, width)

    def talk(number, **more):
        return pltpu.CompilerParams(
            vmem_limit_bytes=VMEM_LIMIT, collective_id=number, has_side_effects=True, **more)

    def gather_all(pieces):
        every = lax.all_gather(pieces, AXES, axis=0, tiled=False).reshape(count_dp, count_t, -1, strip, 384)
        return every.transpose(1, 2, 0, 3, 4).reshape(1, count_t, -1, width, 384)

    if not linked:
        w_att, w_mlp = gather_all(shard[:2]), gather_all(shard[2:])

    vec = once((width,))
    params = pltpu.CompilerParams(dimension_semantics=("arbitrary",), vmem_limit_bytes=VMEM_LIMIT)

    query, key, value, out, attn, x, *rest = pl.pallas_call(
        partial(attend_kernel, windows=windows, padded=padded, keys=keys, size=size, linked=linked),
        grid=(count_t,),
        in_specs=[
            once((local_rows, width)),
        ] + [pl.BlockSpec((blocks, 1, 2, depth, 384), lambda t: (0, t, 0, 0, 0))] * (not linked) + [
            vec, vec, vec, vec, once((64, 128)), once((1, 128)), once(pad_mask.shape[::-1]),
            once((padded, 128)), once((padded, 128)),
        ] + [once((6, strip, 384))] * linked,
        out_specs=[
            pl.BlockSpec((1, 3, rows, 128), lambda t: (t, 0, 0, 0)),
            pl.BlockSpec((1, 3, windows, keys, 128), lambda t: (t, 0, 0, 0, 0)),
            pl.BlockSpec((1, 3, windows, keys, 128), lambda t: (t, 0, 0, 0, 0)),
            pl.BlockSpec((1, rows, 256), lambda t: (t, 0, 0)),
            whole((rows, width)), whole((rows, width)),
        ] + [any_spec, any_spec] * linked,
        out_shape=[
            jax.ShapeDtypeStruct((count_t, 3, rows, 128), BF),
            jax.ShapeDtypeStruct((count_t, 3, windows, keys, 128), BF),
            jax.ShapeDtypeStruct((count_t, 3, windows, keys, 128), BF),
            jax.ShapeDtypeStruct((count_t, rows, 256), BF),
            jax.ShapeDtypeStruct((rows, width), F32),
            jax.ShapeDtypeStruct((rows, width), BF),
        ] + [jax.ShapeDtypeStruct((count_dp, count_t, pieces, strip, 384), BF) for pieces in (2, 4)] * linked,
        scratch_shapes=[
            pltpu.VMEM((rows, width), BF), pltpu.VMEM((rows, 384), BF), pltpu.VMEM((rows, 256), BF),
            pltpu.VMEM((2, 256, 384), BF), pltpu.VMEM((rows, 128), BF), pltpu.VMEM((count_t, 1, 640), F32),
        ]
        + ([pltpu.VMEM((count_dp, count_t, 2, strip, 384), BF)] + gather_scratch() * (1 + MLP_PARTS) + [pltpu.SemaphoreType.DMA((2,))]) * linked,
        compiler_params=talk(2, dimension_semantics=("arbitrary",)) if linked else params,
        name="attend",
    )(
        block_input, *([] if linked else [w_att]), norm1_gain, norm1_bias, q_bias, v_bias, rel, slots, pad_mask.T, feat, amount,
        *([shard] * linked)
    )
    if linked:
        w_att, w_mlp = rest
    w_mlp = w_mlp.reshape(blocks, count_t, 2, 2, depth, 384)

    tiles = 2 * count_t
    mlp_block = pl.BlockSpec((blocks, 1, 2, 1, depth, 384), lambda j: (0, j // 2, 0, j % 2, 0, 0))
    result, gx1, grad_mlp, gbias_up, small2 = pl.pallas_call(
        partial(mlp_kernel, windows=windows, padded=padded),
        grid=(tiles,),
        in_specs=[
            once((rows, width)), once((rows, width)), once((local_rows, width)), once((1, 128)),
            mlp_block, vec, vec, vec, vec, once(fc1_bias.shape),
        ],
        out_specs=[
            whole((local_rows, width)), whole((rows, width)),
            mlp_block,
            pl.BlockSpec((1, 1, 384), lambda j: (j, 0, 0)),
            whole((8, width)),
        ],
        out_shape=[
            jax.ShapeDtypeStruct((local_rows, width), BF),
            jax.ShapeDtypeStruct((rows, width), F32),
            jax.ShapeDtypeStruct((blocks, count_t, 2, 2, depth, 384), BF),
            jax.ShapeDtypeStruct((tiles, 1, 384), F32),
            jax.ShapeDtypeStruct((8, width), F32),
        ],
        scratch_shapes=[
            pltpu.VMEM((rows, width), F32), pltpu.VMEM((rows, width), BF),
            pltpu.VMEM((width, rows), BF), pltpu.VMEM((width, rows), BF),
            pltpu.VMEM((rows, width), F32), pltpu.VMEM((rows, width), F32), pltpu.VMEM((rows, width), BF),
            pltpu.VMEM((tiles, 1, 384), F32),
        ],
        compiler_params=params,
        name="mlp",
    )(x, attn, cotangent, slots, w_mlp, proj_bias, norm2_gain, norm2_bias, fc2_bias, fc1_bias)

    grad_x, grad_att, small1, gbias_att, grel, *rest = pl.pallas_call(
        partial(attend_back_kernel, windows=windows, padded=padded, keys=keys, size=size, linked=linked),
        grid=(count_t,),
        in_specs=[
            once((rows, width)), once((rows, width)),
            pl.BlockSpec((blocks, 1, 2, depth, 384), lambda t: (0, t, 0, 0, 0)),
            vec, vec, once((64, 128)), once((padded, 128)),
            pl.BlockSpec((1, 3, rows, 128), lambda t: (t, 0, 0, 0)),
            pl.BlockSpec((1, 3, windows, keys, 128), lambda t: (t, 0, 0, 0, 0)),
            pl.BlockSpec((1, 3, windows, keys, 128), lambda t: (t, 0, 0, 0, 0)),
            pl.BlockSpec((1, rows, 256), lambda t: (t, 0, 0)),
        ] + [any_spec] * linked,
        out_specs=[
            whole((local_rows, width)),
            pl.BlockSpec((blocks, 1, 2, depth, 384), lambda t: (0, t, 0, 0, 0)),
            whole((8, width)),
            pl.BlockSpec((1, 1, 640), lambda t: (t, 0, 0)),
            whole((128, 128)),
        ] + [whole((4, strip, 384))] * linked,
        out_shape=[
            jax.ShapeDtypeStruct((local_rows, width), BF),
            jax.ShapeDtypeStruct((blocks, count_t, 2, depth, 384), BF),
            jax.ShapeDtypeStruct((8, width), F32),
            jax.ShapeDtypeStruct((count_t, 1, 640), F32),
            jax.ShapeDtypeStruct((128, 128), F32),
        ] + [jax.ShapeDtypeStruct((4, strip, 384), F32)] * linked,
        scratch_shapes=[
            pltpu.VMEM((width, rows), BF), pltpu.VMEM((width, rows), BF), pltpu.VMEM((rows, width), BF),
            pltpu.VMEM((rows, width), F32), pltpu.VMEM((rows, 256), BF),
            pltpu.VMEM((rows, 384), BF), pltpu.VMEM((rows, 256), BF), pltpu.VMEM((3, rows, 128), BF),
            pltpu.VMEM((128, 128), BF),
        ] + (scatter_scratch(4, strip, 384) if linked else []),
        compiler_params=talk(3, dimension_semantics=("arbitrary",)) if linked else params,
        name="attend_back",
    )(
        x, gx1, w_att, norm1_gain, norm1_bias, rel, amount, query, key, value, out,
        *([grad_mlp.reshape(count_dp // 2, 2, count_t, 4, strip, 384)] * linked if linked else [])
    )

    if linked:
        sum_mlp = rest[0]
        count = 36 + 5 * count_t + 3 * tiles + 64
        sum_att, total = pl.pallas_call(
            reduce_kernel,
            in_specs=[any_spec] + [vmem_spec] * 5, out_specs=[vmem_spec, vmem_spec],
            out_shape=[jax.ShapeDtypeStruct((2, strip, 384), F32), jax.ShapeDtypeStruct((count, 128), F32)],
            scratch_shapes=[
                pltpu.VMEM((count, 128), F32), pltpu.VMEM((10, count, 128), F32),
                pltpu.SemaphoreType.DMA((5,)), pltpu.SemaphoreType.DMA((5,)),
            ] + scatter_scratch(2, strip, 384),
            compiler_params=talk(4),
            name="reduce_attention",
        )(grad_att.reshape(count_dp // 2, 2, count_t, 2, strip, 384), small1, small2, gbias_att, gbias_up, grel)
        like = (
            qkv_w, proj_w, fc1_w, fc2_w.T, norm1_gain, norm1_bias, q_bias, v_bias, rel_h, rel_w,
            proj_bias, norm2_gain, norm2_bias, fc1_bias, fc2_bias,
        )
        shapes = [jax.ShapeDtypeStruct(v.shape, F32) for v in like]
        outs = pl.pallas_call(
            partial(unpack_kernel, span=span),
            in_specs=[vmem_spec] * 3, out_specs=[vmem_spec] * len(shapes), out_shape=shapes,
            compiler_params=pltpu.CompilerParams(vmem_limit_bytes=VMEM_LIMIT),
            name="unpack",
        )(total, sum_att, sum_mlp)
        return (result, grad_x, *outs[:3], outs[3].T, *outs[4:])
    parts = [
        small1[:3].reshape(-1, 128), small2[:3].reshape(-1, 128), gbias_att.reshape(-1, 128), gbias_up.reshape(-1, 128), grel[64:],
    ]
    def scatter_all(grads):
        grads = grads.reshape(count_t, -1, count_dp, strip, 384).transpose(2, 0, 1, 3, 4)
        grads = grads.reshape(count_dp * count_t, -1, strip, 384)
        return lax.psum_scatter(grads, AXES, scatter_dimension=0, tiled=False).astype(F32)

    sum_mlp, sum_att = scatter_all(grad_mlp), scatter_all(grad_att)
    small = lax.psum(jnp.concatenate(parts), AXES)
    cuts = np.cumsum([part.shape[0] for part in parts])[:-1]
    small1, small2, gbias_att, gbias_up, grad_rel = jnp.split(small, cuts)
    small1, small2 = small1.reshape(3, width), small2.reshape(3, width)
    gbias_att = gbias_att.reshape(count_t, 1, 640)
    grad_rel = 8.0 * grad_rel[:, :64]
    head_q, head_k = sum_att[0, :, :192], sum_att[0, :, 192:]
    head_v, head_p = sum_att[1, :, :192], sum_att[1, :, 192:]
    return (
        result,
        grad_x,
        jnp.stack([head_q, head_k, head_v]),
        head_p.T,
        jnp.concatenate([sum_mlp[0], sum_mlp[1]], 1),
        jnp.concatenate([sum_mlp[2], sum_mlp[3]], 1).T,
        small1[1],
        small1[2],
        gbias_att[:, 0, :192].reshape(-1),
        gbias_att[:, 0, 384:576].reshape(-1),
        grad_rel[:span][::-1],
        grad_rel[32 : 32 + span][::-1],
        small1[0],
        small2[0],
        small2[1],
        gbias_up.reshape(-1),
        small2[2],
    )


def solution(mesh):
    return jax.shard_map(
        shards,
        mesh=mesh,
        in_specs=(
            P(AXES, None), P(AXES, None), P(), P("dp"),
            P(None, "dp", "tensor"), P("tensor", "dp"), P("dp", "tensor"), P("tensor", "dp"),
        )
        + (P(),) * 11,
        out_specs=(
            P(AXES, None), P(AXES, None),
            P(None, "dp", "tensor"), P("tensor", "dp"), P("dp", "tensor"), P("tensor", "dp"),
        )
        + (P(),) * 11,
        check_vma=False,
    )
```

time: 562 us -> 296 us (0.53)
  waiting for transfers between devices: 263 us -> 0 us
  Pallas kernels: 142 us -> 285 us
  local copies, waits for them, and re-layouts: 78.4 us -> 8.31 us
  blocking collectives: 41.8 us -> 0 us
  other arithmetic: 19.5 us -> 1.54 us
  between operations: 14.2 us -> 0.73 us
    reduce_scatter x2 -> x0, waiting for transfers between devices: 183 us -> none  [the longest x1 139 us: shards(): lax.psum_scatter(grad_mlp, AXES, scatter_dimension=0, tiled=False)]
    all_gather x2 -> x0, waiting for transfers between devices: 79.3 us -> none  [the longest x1 43.2 us: shards(): lax.all_gather(shard[2:], AXES, axis=0, tiled=False)]
    pallas_call x1, Pallas kernels: 35.1 us -> 105 us  [shards(): pl.pallas_call(partial(attend_kernel, windows=windows, padded=padded, key...]
    pallas_call x1 -> x3, Pallas kernels: 44.7 us -> 102 us  [the longest x1 54.4 us: shards(): pl.pallas_call(reduce_kernel, in_specs=[any_spec] + [vmem_spec] * 5, out_...]
    psum x1 -> x0, blocking collectives: 41.8 us -> none  [shards(): lax.psum((small1[:3], small2[:3], gbias_att, gbias_up, grad_rel), AXES)]
    transpose x3 -> x0, local copies, waits for them, and re-layouts: 17.6 us -> none  [the longest x1 8.89 us: shards(): gathered_m.transpose(2, 1, 0, 3, 4).reshape(2, 2, count_t, width, 384)]
    pallas_call x1, Pallas kernels: 61.9 us -> 78 us  [shards(): pl.pallas_call(partial(attend_back_kernel, windows=windows, padded=padded...]
    slice x11 -> x0, local copies, waits for them, and re-layouts: 12.9 us -> none  [the longest x2 7.5 us: shards(): w_down = w_mlp[1].reshape(count_t * 2, width, 384)]
  transfers between devices with their start and end apart: 4 -> 0, of which waited for: 4 -> 0; matrix products, arithmetic and copies ran while one was open for 11% -> 0% of each run, Pallas kernels for 6% -> 0%
where the time goes in v2:
time: 296 us
  Pallas kernels  285 us (96%)
  local copies, waits for them, and re-layouts  8.31 us (3%)
    pallas_call x1, Pallas kernels, shards(): pl.pallas_call(partial(attend_kernel, windows=windows, padded=padded, key...  105 us
    pallas_call x1, Pallas kernels, shards(): pl.pallas_call(partial(attend_back_kernel, windows=windows, padded=padded...  78 us
    pallas_call x1, Pallas kernels, shards(): pl.pallas_call(reduce_kernel, in_specs=[any_spec] + [vmem_spec] * 5, out_...  54.4 us
    pallas_call x1, Pallas kernels, shards(): pl.pallas_call(partial(mlp_kernel, windows=windows, padded=padded), grid=...  45.1 us

profile of v2, /device:TPU:1, one launch (start us, length us, event | category | flops | bytes accessed | tf_op | source)
XLA Modules:
  0.0 295.9 jit_solution(12122858282214997993)
XLA Ops:
  0.7 1.2 pad_bitcast_fusion.refs_6_.slots_ref
  1.8 1.4 select_maximum_fusion.refs_5_
  3.2 0.9 copy.38
  4.1 0.9 slice_bitcast_fusion.2
  4.9 0.1 fusion.2
  5.0 0.1 fusion.3
  5.1 0.9 bitcast_dynamic-update-slice_fusion.1
  6.0 0.9 bitcast_dynamic-update-slice_fusion
  6.9 0.9 fusion.1
  7.8 0.9 fusion.refs_10_
  8.7 0.0 copy-start.1
  8.8 0.8 copy-done.1
  9.5 105.5 %attend.1 = (bf16[4,3,832,128]{3,2,1,0:T(8,128)(2,1)}, bf16[4,3,4,256,128]{4,3,2,1,0:T(8,128)(2,1)}, bf16[4,3,4,256,128]{4,3,2,1,0:T(8,128)(2,1)}, bf16[4,832,25...) custom-call(bf16[784,768]{1,0:T(8,128)(2,1)} %refs_0_.1, ...), custom_call_target="tpu_custom_call" | custom-call | tf_op jit(solution)/shard_map/attend/pallas_call | solution.py:864
  115.0 45.1 %mlp.1 = (bf16[784,768]{1,0:T(8,128)(2,1)}, f32[832,768]{1,0:T(8,128)}, bf16[8,4,2,2,96,384]{5,4,3,2,1,0:T(8,128)(2,1)}, f32[8,1,384]{2,1,0:T(1,128)}, f32[8,768]{1,0:T(8,128)}) custom-call(bf16[832,768]{1,0:T(8,128)(2,1)} %get-tuple-element.53.x_ref.refs_0_, f32[832,768]{1,0:T(8,128)} %get-tuple-element.54.attn_ref, bf16[784,768]{1,0:T(8,128)(2,1)} %cotangent_ref.1, ...), custom_call_target="tpu_custom_call" | custom-call | tf_op jit(solution)/shard_map/mlp/pallas_call | solution.py:905
  160.1 78.0 %attend_back.1 = (bf16[784,768]{1,0:T(8,128)(2,1)}, bf16[8,4,2,96,384]{4,3,2,1,0:T(8,128)(2,1)}, f32[8,768]{1,0:T(8,128)}, f32[4,1,640]{2,1,0:T(1,128)}, f32[128,128]{1,0:T(8,128)}, /*index=5*/f32[4,96,384]{2,1,0:T(8,128)}) custom-call(bf16[832,768]{1,0:T(8,128)(2,1)} %get-tuple-element.53.x_ref.refs_0_, f32[832,768]{1,0:T(8,128)} %get-tuple-element.57.refs_1_, ...), custom_call_target="tpu_custom_call" | custom-call | tf_op jit(solution)/shard_map/attend_back/pallas_call | solution.py:935
  238.1 0.0 copy-start
  238.1 54.4 %reduce_attention.1 = (f32[2,96,384]{2,1,0:T(8,128)}, f32[144,128]{1,0:T(8,128)}) custom-call(bf16[4,2,4,2,96,384]{5,4,3,2,1,0:T(8,128)(2,1)} %bitcast.37, f32[8,768]{1,0:T(8,128)} %get-tuple-element.66.small1_ref, f32[8,768]{1,0:T(8,128)} %get-tuple-element.67.small2_ref, f32[4,1,640]{2,1,0:T(1,128)} %get-tuple-element.68.gbias_att_ref, ...), custom_call_target="tpu_custom_call" | custom-call | tf_op jit(solution)/shard_map/reduce_attention/pallas_call | solution.py:977
  292.6 2.3 unpack.1
  294.8 0.0 copy-done
  294.9 1.0 copy.45
Async XLA Ops:
  8.7 0.8 copy-start.1
  238.1 56.8 %copy-start = (bf16[784,768]{1,0:T(8,128)(2,1)S(1)}, bf16[784,768]{1,0:T(8,128)(2,1)}, u32[]{:S(2)}) copy-start(bf16[784,768]{1,0:T(8,128)(2,1)} %get-tuple-element.110) | copy-start | bytes 3612676

commit v3 on v2

--- a/solution.py
+++ b/solution.py
@@ -14,9 +14,9 @@
 F32, BF = jnp.float32, jnp.bfloat16
 AXES = ("dp", "tensor")
 VMEM_LIMIT = 60 * 1024 * 1024
-MLP_PARTS = 1
-MLP_BEGIN = (11,)
-MLP_SLOTS = tuple(int(i * 2.8) for i in range(15))
+MLP_BEGIN = 11
+MLP_SLOTS = tuple(range(3, 48, 3))
+SUM_SLOTS = (3, 3, 6, 6, 9, 12, 15, 15, 18, 18, 21, 21, 24, 24, 27, 27, 30, 33, 36)
 
 
 def nn(left, right):
@@ -47,15 +47,13 @@
     return inverse * inner
 
 
-def spread_rows(source_ref, target_ref, windows, padded, scale=None):
-    length = source_ref.shape[0] // windows
-    for w in range(windows):
-        tail = w * padded + length // 16 * 16
-        target_ref[tail : w * padded + padded, :] = jnp.zeros((w * padded + padded - tail, target_ref.shape[1]), target_ref.dtype)
-        values = source_ref[w * length : w * length + length, :]
-        if scale is not None:
-            values = jnp.where(scale(w) > 0.5, values.astype(F32), 0.0).astype(values.dtype)
-        target_ref[w * padded : w * padded + length, :] = values
+def spread_rows(source_ref, target_ref, w, length, padded, live=None):
+    tail = w * padded + length // 16 * 16
+    target_ref[tail : w * padded + padded, :] = jnp.zeros((w * padded + padded - tail, target_ref.shape[1]), target_ref.dtype)
+    values = source_ref[w * length : w * length + length, :]
+    if live is not None:
+        values = jnp.where(live > 0.5, values.astype(F32), 0.0).astype(values.dtype)
+    target_ref[w * padded : w * padded + length, :] = values
 
 
 def row(ref):
@@ -240,9 +238,8 @@
         near = [lambda k=k: self.from_near(k) for k in range(4)]
         line = [lambda k=k: self.from_line(k) for k in range(4)]
         self.steps = [
-            [self.begin], [core[1, 1], core[1, 0]], [core[0, 1], core[0, 0]], [far[1][3]], [far[1][2]],
-            [far[1][1], near[3]], [far[1][0], near[2]], [far[0][3], near[1]], [far[0][2], line[3]], [near[0], far[0][1]],
-            [line[2]], [far[0][0]], [line[1]], [], [],
+            core[1, 1], core[1, 0], core[0, 1], core[0, 0], far[1][3], far[1][2], far[1][1], near[3], far[1][0], near[2],
+            far[0][3], near[1], far[0][2], line[3], near[0], far[0][1], line[2], far[0][0], line[1],
         ]
         self.last = line[0]
 
@@ -416,17 +413,10 @@
             small_ref[row : row + 1, :] = ref[index[0], 0:1, index[2] : index[2] + 128]
     small_ref[small_ref.shape[0] - 64 :, :] = grel_ref[64:, :]
     exchange(0).start()
-    for step in scatter.steps[1]:
+    for number, step in enumerate(scatter.steps):
         step()
-    fold(0)
-    for step in scatter.steps[2]:
-        step()
-    fold(1)
-    for number, steps in enumerate(scatter.steps[3:]):
-        for step in steps:
-            step()
-        if number in (0, 2, 4):
-            fold(2 + number // 2)
+        if number in (1, 3, 4, 7, 10):
+            fold((1, 3, 4, 7, 10).index(number))
     scatter.finish()
     for index in range(5):
         exchange(index).wait_send()
@@ -437,27 +427,22 @@
     duties = {}
     refs = list(refs)
     if linked:
-        own_ref, att_ref, mlp_ref, w_ref, keep_sem = refs[10], refs[17], refs[18], refs[25], refs[-1]
+        own_ref, more_ref, att_ref, mlp_ref, w_ref, keep_sem = refs[10], refs[11], refs[18], refs[19], refs[26], refs[-1]
         at = Place(4)
-        att = Gather(at, own_ref.at[:2], w_ref, *refs[26:28])
-        share = 4 // MLP_PARTS
-        mlp = [
-            Gather(at, own_ref.at[2 + i * share : 2 + i * share + share], mlp_ref, *refs[28 + 2 * i : 30 + 2 * i], i * share, share)
-            for i in range(MLP_PARTS)
-        ]
-        todo = [act for acts in zip(*[part.steps for part in mlp]) for act in acts]
-        mine = pltpu.make_async_copy(own_ref.at[2:], mlp_ref.at[at.dp, at.tensor], keep_sem.at[0])
+        att = Gather(at, own_ref, w_ref, *refs[27:29])
+        mlp = Gather(at, more_ref, mlp_ref, *refs[29:31])
+        mine = pltpu.make_async_copy(more_ref, mlp_ref.at[at.dp, at.tensor], keep_sem.at[0])
         keep = pltpu.make_async_copy(w_ref, att_ref, keep_sem.at[1])
-        refs = refs[:1] + [w_ref] + refs[1:10] + refs[11:17] + refs[19:25]
+        refs = refs[:1] + [w_ref] + refs[1:10] + refs[12:18] + refs[20:26]
 
         @pl.when(step == 0)
         def _():
             at.greet()
             att.begin()
-            w_ref[at.dp, at.tensor] = own_ref[:2]
+            w_ref[at.dp, at.tensor] = own_ref[...]
             mine.start()
 
-        duties = {slot: [todo[i] for i in range(len(todo)) if MLP_SLOTS[i] == slot] for slot in MLP_SLOTS}
+        duties = {slot: [act for act, when in zip(mlp.steps, MLP_SLOTS) if when == slot] for slot in MLP_SLOTS}
     (
         raw_ref, w_ref, gain_ref, shift_ref, query_bias_ref, value_bias_ref, rel_ref, slots_ref, pad_ref, feat_ref, amount_ref,
         query_ref, key_ref, value_ref, out_ref, acc_ref, x_ref,
@@ -466,48 +451,58 @@
 
     @pl.when(step == 0)
     def _():
-        length = pad_ref.shape[0]
-        spread_rows(raw_ref, x_ref, windows, padded)
-        normed, _ = normed_of(x_ref[...].astype(F32))
-        h1_ref[...] = (normed * row(gain_ref) + row(shift_ref)).astype(BF)
-        acc_ref[...] = jnp.zeros_like(acc_ref)
-
+        length, count = pad_ref.shape
         span = 2 * size - 1
-        place = lax.broadcasted_iota(jnp.int32, (64, 128), 0)
-        lane = lanes_of((64, 128))
-        wanted = jnp.where(place < span, 64 + span - 1 - place, jnp.where(place < 2 * span, 96 + 2 * span - 1 - place, -1))
-        chosen = jnp.where(lane == wanted, 1.0, 0.0).astype(BF)
-        rel = rel_ref[...]
-        high = rel.astype(BF)
-        rest = (rel - high.astype(F32)).astype(BF)
-        table_ref[...] = jnp.zeros_like(table_ref)
-        for number, piece in enumerate((high, rest)):
-            turned = tn(piece, chosen)[:64].astype(BF)
-            for head in range(3):
-                table_ref[number, head * 64 : head * 64 + 64, head * 128 : head * 128 + 128] = turned
-
         part = lax.axis_index("tensor")
-        count = pad_ref.shape[1]
-        picked = jnp.where(lax.broadcasted_iota(jnp.int32, (count, 128), 0) == slots_ref[...], 1.0, 0.0).astype(BF)
-        usable = nn(pad_ref[...].astype(F32).astype(BF), picked)
-        for w in range(windows):
-            mask = jnp.where(of_slot(usable, part * windows + w) > 0.5, 0.0, NEGATIVE)
-            start = w * padded
-            key_feat_ref[start : start + padded, :] = feat_ref[...]
-            key_feat_ref[start : start + length, :] = jnp.where(
-                lanes_of((length, 128)) == 79, mask, feat_ref[:length, :].astype(F32)).astype(BF)
-        bias_ref[...] = jnp.zeros_like(bias_ref)
-        for t in range(bias_ref.shape[0]):
-            bias_ref[t, 0:1, 0:192] = row(query_bias_ref)[:, t * 192 : t * 192 + 192]
-            bias_ref[t, 0:1, 384:576] = row(value_bias_ref)[:, t * 192 : t * 192 + 192]
-
+
+        def norm_rows(w):
+            spread_rows(raw_ref, x_ref, w, length, padded)
+            here = slice(w * padded, w * padded + padded)
+            normed, _ = normed_of(x_ref[here, :].astype(F32))
+            h1_ref[here, :] = (normed * row(gain_ref) + row(shift_ref)).astype(BF)
+            acc_ref[here, :] = jnp.zeros((padded, acc_ref.shape[1]), F32)
+
+        def tables():
+            place = lax.broadcasted_iota(jnp.int32, (64, 128), 0)
+            lane = lanes_of((64, 128))
+            wanted = jnp.where(place < span, 64 + span - 1 - place, jnp.where(place < 2 * span, 96 + 2 * span - 1 - place, -1))
+            chosen = jnp.where(lane == wanted, 1.0, 0.0).astype(BF)
+            rel = rel_ref[...]
+            high = rel.astype(BF)
+            rest = (rel - high.astype(F32)).astype(BF)
+            table_ref[...] = jnp.zeros_like(table_ref)
+            for number, piece in enumerate((high, rest)):
+                turned = tn(piece, chosen)[:64].astype(BF)
+                for head in range(3):
+                    table_ref[number, head * 64 : head * 64 + 64, head * 128 : head * 128 + 128] = turned
+            bias_ref[...] = jnp.zeros_like(bias_ref)
+            for t in range(bias_ref.shape[0]):
+                bias_ref[t, 0:1, 0:192] = row(query_bias_ref)[:, t * 192 : t * 192 + 192]
+                bias_ref[t, 0:1, 384:576] = row(value_bias_ref)[:, t * 192 : t * 192 + 192]
+
+        def features():
+            picked = jnp.where(lax.broadcasted_iota(jnp.int32, (count, 128), 0) == slots_ref[...], 1.0, 0.0).astype(BF)
+            usable = nn(pad_ref[...].astype(F32).astype(BF), picked)
+            for w in range(windows):
+                mask = jnp.where(of_slot(usable, part * windows + w) > 0.5, 0.0, NEGATIVE)
+                start = w * padded
+                key_feat_ref[start : start + padded, :] = feat_ref[...]
+                key_feat_ref[start : start + length, :] = jnp.where(
+                    lanes_of((length, 128)) == 79, mask, feat_ref[:length, :].astype(F32)).astype(BF)
+
+        chores = [lambda w=w: norm_rows(w) for w in range(windows)] + [tables, features]
         if linked:
             for number, act in enumerate(att.steps):
                 act()
-                if number in MLP_BEGIN:
-                    mlp[MLP_BEGIN.index(number)].begin()
+                if number == MLP_BEGIN:
+                    mlp.begin()
+                if number < len(chores):
+                    chores[number]()
             att.arrive()
             keep.start()
+        else:
+            for chore in chores:
+                chore()
 
     h1 = h1_ref[...]
     chunk = step if linked else 0
@@ -576,12 +571,15 @@
 
         @pl.when(step == pl.num_programs(0) - 1)
         def _():
-            for part in mlp:
-                part.arrive()
+            for slot in duties:
+                if slot >= 48:
+                    for act in duties[slot]:
+                        act()
+            mlp.arrive()
             mine.wait()
             keep.wait()
-            for part in [att] + mlp:
-                part.finish()
+            att.finish()
+            mlp.finish()
 
 
 def mlp_kernel(
@@ -591,13 +589,14 @@
     *, windows, padded,
 ):
     first = lax.axis_index("tensor") * windows
-    columns = w_ref.shape[5]
+    columns = w_ref.shape[4]
     step = pl.program_id(0)
     last = pl.num_programs(0) - 1
 
     @pl.when(step == 0)
     def _():
-        spread_rows(cotangent_ref, gy_ref, windows, padded, lambda w: alive_of(slots_ref, first + w))
+        for w in range(windows):
+            spread_rows(cotangent_ref, gy_ref, w, cotangent_ref.shape[0] // windows, padded, alive_of(slots_ref, first + w))
         x1 = x_ref[...].astype(F32) + (attn_ref[...] + row(bias_proj_ref))
         x1_ref[...] = x1
         normed, _ = normed_of(x1)
@@ -610,8 +609,8 @@
         y_ref[...] = jnp.zeros_like(y_ref)
         dh_ref[...] = jnp.zeros_like(dh_ref)
 
-    up, down = flat(w_ref[:, 0, 0, 0]), flat(w_ref[:, 0, 1, 0])
-    strips = (grad_ref.shape[0], grad_ref.shape[4], up.shape[1])
+    up, down = flat(w_ref[:, 0, 0]), flat(w_ref[:, 0, 1])
+    strips = (grad_ref.shape[0], grad_ref.shape[3], columns)
     upper = nn(h2_ref[...], up) + bias_ref[step]
     half = 0.5 * (1.0 + lax.erf(upper * np.float32(np.sqrt(0.5))))
     slope = half + upper * (np.float32(1.0 / np.sqrt(2 * np.pi)) * jnp.exp(-0.5 * upper * upper))
@@ -619,8 +618,8 @@
     grad_upper = (nn(gy_ref[...], down) * slope).astype(BF)
     y_ref[...] += nt(active, down)
     dh_ref[...] += nt(grad_upper, up)
-    grad_ref[:, 0, 1, 0] = nn(gyt_ref[...], active).astype(BF).reshape(strips)
-    grad_ref[:, 0, 0, 0] = nn(h2t_ref[...], grad_upper).astype(BF).reshape(strips)
+    grad_ref[:, 0, 1] = nn(gyt_ref[...], active).astype(BF).reshape(strips)
+    grad_ref[:, 0, 0] = nn(h2t_ref[...], grad_upper).astype(BF).reshape(strips)
     gbias_up_ref[0] = jnp.sum(grad_upper.astype(F32), 0, keepdims=True)
 
     @pl.when(step == last)
@@ -680,10 +679,6 @@
     kept = (lane >= 64) & (field < 14)
 
     def window(w, carry):
-        if linked:
-            for number in range(1, len(scatter.steps)):
-                for action in scatter.steps[number]:
-                    pl.when(step * windows + w == number)(action)
         rows = pl.ds(pl.multiple_of(w * padded, 16), padded)
         do = do_ref[rows, :].astype(F32)
         out = out_ref[0, rows, :].astype(F32)
@@ -696,6 +691,10 @@
         ]
         gq, gk, gv = [], [], []
         for head in range(3):
+            if linked:
+                for slot, act in zip(SUM_SLOTS, scatter.steps):
+                    if slot % 3 == head:
+                        pl.when(step * windows + w == slot // 3)(act)
             delta = -sums[head]
             first = delta.astype(BF).astype(F32)
             grad_out = jnp.where(low, grads[head], jnp.where(lane == 64, first, jnp.where(lane == 65, delta - first, 0.0))).astype(BF)
@@ -744,6 +743,9 @@
         small_ref[2:3, :] = jnp.sum(dh, 0, keepdims=True)
         small_ref[3:8, :] = jnp.zeros_like(small_ref[3:8, :])
         if linked:
+            for slot, act in zip(SUM_SLOTS, scatter.steps):
+                if slot >= 48:
+                    act()
             scatter.finish()
 
 
@@ -757,10 +759,8 @@
     qkv_ref[1] = att_ref[0, :, 192:]
     qkv_ref[2] = att_ref[1, :, :192]
     proj_ref[...] = att_ref[1, :, 192:].T
-    up_ref[:, :384] = mlp_ref[0]
-    up_ref[:, 384:] = mlp_ref[1]
-    down_ref[:, :384] = mlp_ref[2]
-    down_ref[:, 384:] = mlp_ref[3]
+    up_ref[...] = mlp_ref[0]
+    down_ref[...] = mlp_ref[1]
     for first, ref in ((0, proj_bias_ref), (6, gain1_ref), (12, shift1_ref), (18, gain2_ref), (24, shift2_ref), (30, down_bias_ref), (56, up_bias_ref)):
         for lane in range(0, ref.shape[0], 128):
             ref[pl.ds(lane, 128)] = total_ref[first + lane // 128]
@@ -833,16 +833,9 @@
     span = rel_h.shape[0]
 
     q_w, k_w, v_w = qkv_w[0], qkv_w[1], qkv_w[2]
-    shard = jnp.stack(
-        [
-            jnp.concatenate([q_w, k_w], 1),
-            jnp.concatenate([v_w, proj_w.T], 1),
-            fc1_w[:, :384],
-            fc1_w[:, 384:],
-            fc2_w.T[:, :384],
-            fc2_w.T[:, 384:],
-        ]
-    )
+    shard_att = jnp.stack([jnp.concatenate([q_w, k_w], 1), jnp.concatenate([v_w, proj_w.T], 1)])
+    shard_mlp = jnp.stack([fc1_w, fc2_w.T])
+    columns = fc1_w.shape[1]
     linked = count_dp == 8 and count_t == 4 and strip % 16 == 0 and windows == 4
     any_spec, vmem_spec = pl.BlockSpec(memory_space=pl.ANY), pl.BlockSpec(memory_space=pltpu.VMEM)
     blocks, depth = (count_dp, strip) if linked else (1, width)
@@ -852,11 +845,11 @@
             vmem_limit_bytes=VMEM_LIMIT, collective_id=number, has_side_effects=True, **more)
 
     def gather_all(pieces):
-        every = lax.all_gather(pieces, AXES, axis=0, tiled=False).reshape(count_dp, count_t, -1, strip, 384)
-        return every.transpose(1, 2, 0, 3, 4).reshape(1, count_t, -1, width, 384)
+        every = lax.all_gather(pieces, AXES, axis=0, tiled=False).reshape(count_dp, count_t, *pieces.shape)
+        return every.transpose(1, 2, 0, 3, 4).reshape(1, count_t, 2, width, pieces.shape[2])
 
     if not linked:
-        w_att, w_mlp = gather_all(shard[:2]), gather_all(shard[2:])
+        w_att, w_mlp = gather_all(shard_att), gather_all(shard_mlp)
 
     vec = once((width,))
     params = pltpu.CompilerParams(dimension_semantics=("arbitrary",), vmem_limit_bytes=VMEM_LIMIT)
@@ -869,7 +862,7 @@
         ] + [pl.BlockSpec((blocks, 1, 2, depth, 384), lambda t: (0, t, 0, 0, 0))] * (not linked) + [
             vec, vec, vec, vec, once((64, 128)), once((1, 128)), once(pad_mask.shape[::-1]),
             once((padded, 128)), once((padded, 128)),
-        ] + [once((6, strip, 384))] * linked,
+        ] + [once((2, strip, 384)), once((2, strip, columns))] * linked,
         out_specs=[
             pl.BlockSpec((1, 3, rows, 128), lambda t: (t, 0, 0, 0)),
             pl.BlockSpec((1, 3, windows, keys, 128), lambda t: (t, 0, 0, 0, 0)),
@@ -884,27 +877,25 @@
             jax.ShapeDtypeStruct((count_t, rows, 256), BF),
             jax.ShapeDtypeStruct((rows, width), F32),
             jax.ShapeDtypeStruct((rows, width), BF),
-        ] + [jax.ShapeDtypeStruct((count_dp, count_t, pieces, strip, 384), BF) for pieces in (2, 4)] * linked,
+        ] + [jax.ShapeDtypeStruct((count_dp, count_t, 2, strip, n), BF) for n in (384, columns)] * linked,
         scratch_shapes=[
             pltpu.VMEM((rows, width), BF), pltpu.VMEM((rows, 384), BF), pltpu.VMEM((rows, 256), BF),
             pltpu.VMEM((2, 256, 384), BF), pltpu.VMEM((rows, 128), BF), pltpu.VMEM((count_t, 1, 640), F32),
         ]
-        + ([pltpu.VMEM((count_dp, count_t, 2, strip, 384), BF)] + gather_scratch() * (1 + MLP_PARTS) + [pltpu.SemaphoreType.DMA((2,))]) * linked,
+        + ([pltpu.VMEM((count_dp, count_t, 2, strip, 384), BF)] + gather_scratch() * 2 + [pltpu.SemaphoreType.DMA((2,))]) * linked,
         compiler_params=talk(2, dimension_semantics=("arbitrary",)) if linked else params,
         name="attend",
     )(
         block_input, *([] if linked else [w_att]), norm1_gain, norm1_bias, q_bias, v_bias, rel, slots, pad_mask.T, feat, amount,
-        *([shard] * linked)
+        *([shard_att, shard_mlp] * linked)
     )
     if linked:
         w_att, w_mlp = rest
-    w_mlp = w_mlp.reshape(blocks, count_t, 2, 2, depth, 384)
-
-    tiles = 2 * count_t
-    mlp_block = pl.BlockSpec((blocks, 1, 2, 1, depth, 384), lambda j: (0, j // 2, 0, j % 2, 0, 0))
+
+    mlp_block = pl.BlockSpec((blocks, 1, 2, depth, columns), lambda j: (0, j, 0, 0, 0))
     result, gx1, grad_mlp, gbias_up, small2 = pl.pallas_call(
         partial(mlp_kernel, windows=windows, padded=padded),
-        grid=(tiles,),
+        grid=(count_t,),
         in_specs=[
             once((rows, width)), once((rows, width)), once((local_rows, width)), once((1, 128)),
             mlp_block, vec, vec, vec, vec, once(fc1_bias.shape),
@@ -912,21 +903,21 @@
         out_specs=[
             whole((local_rows, width)), whole((rows, width)),
             mlp_block,
-            pl.BlockSpec((1, 1, 384), lambda j: (j, 0, 0)),
+            pl.BlockSpec((1, 1, columns), lambda j: (j, 0, 0)),
             whole((8, width)),
         ],
         out_shape=[
             jax.ShapeDtypeStruct((local_rows, width), BF),
             jax.ShapeDtypeStruct((rows, width), F32),
-            jax.ShapeDtypeStruct((blocks, count_t, 2, 2, depth, 384), BF),
-            jax.ShapeDtypeStruct((tiles, 1, 384), F32),
+            jax.ShapeDtypeStruct((blocks, count_t, 2, depth, columns), BF),
+            jax.ShapeDtypeStruct((count_t, 1, columns), F32),
             jax.ShapeDtypeStruct((8, width), F32),
         ],
         scratch_shapes=[
             pltpu.VMEM((rows, width), F32), pltpu.VMEM((rows, width), BF),
             pltpu.VMEM((width, rows), BF), pltpu.VMEM((width, rows), BF),
             pltpu.VMEM((rows, width), F32), pltpu.VMEM((rows, width), F32), pltpu.VMEM((rows, width), BF),
-            pltpu.VMEM((tiles, 1, 384), F32),
+            pltpu.VMEM((count_t, 1, columns), F32),
         ],
         compiler_params=params,
         name="mlp",
@@ -950,30 +941,30 @@
             whole((8, width)),
             pl.BlockSpec((1, 1, 640), lambda t: (t, 0, 0)),
             whole((128, 128)),
-        ] + [whole((4, strip, 384))] * linked,
+        ] + [whole((2, strip, columns))] * linked,
         out_shape=[
             jax.ShapeDtypeStruct((local_rows, width), BF),
             jax.ShapeDtypeStruct((blocks, count_t, 2, depth, 384), BF),
             jax.ShapeDtypeStruct((8, width), F32),
             jax.ShapeDtypeStruct((count_t, 1, 640), F32),
             jax.ShapeDtypeStruct((128, 128), F32),
-        ] + [jax.ShapeDtypeStruct((4, strip, 384), F32)] * linked,
+        ] + [jax.ShapeDtypeStruct((2, strip, columns), F32)] * linked,
         scratch_shapes=[
             pltpu.VMEM((width, rows), BF), pltpu.VMEM((width, rows), BF), pltpu.VMEM((rows, width), BF),
             pltpu.VMEM((rows, width), F32), pltpu.VMEM((rows, 256), BF),
             pltpu.VMEM((rows, 384), BF), pltpu.VMEM((rows, 256), BF), pltpu.VMEM((3, rows, 128), BF),
             pltpu.VMEM((128, 128), BF),
-        ] + (scatter_scratch(4, strip, 384) if linked else []),
+        ] + (scatter_scratch(2, strip, columns) if linked else []),
         compiler_params=talk(3, dimension_semantics=("arbitrary",)) if linked else params,
         name="attend_back",
     )(
         x, gx1, w_att, norm1_gain, norm1_bias, rel, amount, query, key, value, out,
-        *([grad_mlp.reshape(count_dp // 2, 2, count_t, 4, strip, 384)] * linked if linked else [])
+        *([grad_mlp.reshape(count_dp // 2, 2, count_t, 2, strip, columns)] * linked if linked else [])
     )
 
     if linked:
         sum_mlp = rest[0]
-        count = 36 + 5 * count_t + 3 * tiles + 64
+        count = 36 + 5 * count_t + fc1_bias.shape[0] // 128 + 64
         sum_att, total = pl.pallas_call(
             reduce_kernel,
             in_specs=[any_spec] + [vmem_spec] * 5, out_specs=[vmem_spec, vmem_spec],
@@ -1001,8 +992,8 @@
         small1[:3].reshape(-1, 128), small2[:3].reshape(-1, 128), gbias_att.reshape(-1, 128), gbias_up.reshape(-1, 128), grel[64:],
     ]
     def scatter_all(grads):
-        grads = grads.reshape(count_t, -1, count_dp, strip, 384).transpose(2, 0, 1, 3, 4)
-        grads = grads.reshape(count_dp * count_t, -1, strip, 384)
+        grads = grads.reshape(count_t, 2, count_dp, strip, grads.shape[4]).transpose(2, 0, 1, 3, 4)
+        grads = grads.reshape(count_dp * count_t, *grads.shape[2:])
         return lax.psum_scatter(grads, AXES, scatter_dimension=0, tiled=False).astype(F32)
 
     sum_mlp, sum_att = scatter_all(grad_mlp), scatter_all(grad_att)
@@ -1019,8 +1010,8 @@
         grad_x,
         jnp.stack([head_q, head_k, head_v]),
         head_p.T,
-        jnp.concatenate([sum_mlp[0], sum_mlp[1]], 1),
-        jnp.concatenate([sum_mlp[2], sum_mlp[3]], 1).T,
+        sum_mlp[0],
+        sum_mlp[1].T,
         small1[1],
         small1[2],
         gbias_att[:, 0, :192].reshape(-1),

time: 296 us -> 271 us (0.916)
  Pallas kernels: 285 us -> 262 us
  local copies, waits for them, and re-layouts: 8.31 us -> 3.94 us
    pallas_call x1, Pallas kernels: 105 us -> 93 us  [shards(): pl.pallas_call(partial(attend_kernel, windows=windows, padded=padded, key...]
    pallas_call x1, Pallas kernels: 45.1 us -> 37 us  [shards(): pl.pallas_call(partial(mlp_kernel, windows=windows, padded=padded), grid=...]
    unnamed x9 -> x4, local copies, waits for them, and re-layouts: 5.37 us -> 1.91 us
where the time goes in v3:
time: 271 us
  Pallas kernels  262 us (97%)
  local copies, waits for them, and re-layouts  3.94 us (1%)
  other arithmetic  3.86 us (1%)
    pallas_call x1, Pallas kernels, shards(): pl.pallas_call(partial(attend_kernel, windows=windows, padded=padded, key...  93 us
    pallas_call x1, Pallas kernels, shards(): pl.pallas_call(partial(attend_back_kernel, windows=windows, padded=padded...  75.5 us
    pallas_call x1, Pallas kernels, shards(): pl.pallas_call(reduce_kernel, in_specs=[any_spec] + [vmem_spec] * 5, out_...  54.5 us
    pallas_call x1, Pallas kernels, shards(): pl.pallas_call(partial(mlp_kernel, windows=windows, padded=padded), grid=...  37 us

profile of v3, /device:TPU:1, one launch (start us, length us, event | category | flops | bytes accessed | tf_op | source)
XLA Modules:
  0.0 270.8 jit_solution(9908021542491356652)
XLA Ops:
  0.7 1.2 pad_bitcast_fusion.refs_6_.slots_ref
  1.8 1.4 select_maximum_fusion.refs_5_
  3.2 0.9 copy.38
  4.1 0.9 slice_bitcast_fusion.2
  4.9 0.1 maximum_bitcast_fusion
  5.0 0.7 pad_maximum_fusion.1.refs_10_
  5.7 1.7 pad_maximum_fusion.refs_11_
  7.4 93.0 %attend.1 = (bf16[4,3,832,128]{3,2,1,0:T(8,128)(2,1)}, bf16[4,3,4,256,128]{4,3,2,1,0:T(8,128)(2,1)}, bf16[4,3,4,256,128]{4,3,2,1,0:T(8,128)(2,1)}, bf16[4,832,25...) custom-call(bf16[784,768]{1,0:T(8,128)(2,1)} %refs_0_.1, ...), custom_call_target="tpu_custom_call" | custom-call | tf_op jit(solution)/shard_map/attend/pallas_call | solution.py:857
  100.4 37.0 %mlp.1 = (bf16[784,768]{1,0:T(8,128)(2,1)}, f32[832,768]{1,0:T(8,128)}, bf16[8,4,2,96,768]{4,3,2,1,0:T(8,128)(2,1)}, f32[4,1,768]{2,1,0:T(1,128)}, f32[8,768]{1,0:T(8,128)}) custom-call(bf16[832,768]{1,0:T(8,128)(2,1)} %get-tuple-element.53.x_ref.refs_0_, f32[832,768]{1,0:T(8,128)} %get-tuple-element.54.attn_ref, bf16[784,768]{1,0:T(8,128)(2,1)} %cotangent_ref.1, ...), custom_call_target="tpu_custom_call" | custom-call | tf_op jit(solution)/shard_map/mlp/pallas_call | solution.py:896
  137.4 75.5 %attend_back.1 = (bf16[784,768]{1,0:T(8,128)(2,1)}, bf16[8,4,2,96,384]{4,3,2,1,0:T(8,128)(2,1)}, f32[8,768]{1,0:T(8,128)}, f32[4,1,640]{2,1,0:T(1,128)}, f32[128,128]{1,0:T(8,128)}, /*index=5*/f32[2,96,768]{2,1,0:T(8,128)}) custom-call(bf16[832,768]{1,0:T(8,128)(2,1)} %get-tuple-element.53.x_ref.refs_0_, f32[832,768]{1,0:T(8,128)} %get-tuple-element.57.refs_1_, ...), custom_call_target="tpu_custom_call" | custom-call | tf_op jit(solution)/shard_map/attend_back/pallas_call | solution.py:926
  213.0 0.0 copy-start
  213.0 54.5 %reduce_attention.1 = (f32[2,96,384]{2,1,0:T(8,128)}, f32[144,128]{1,0:T(8,128)}) custom-call(bf16[4,2,4,2,96,384]{5,4,3,2,1,0:T(8,128)(2,1)} %bitcast.22, f32[8,768]{1,0:T(8,128)} %get-tuple-element.66.small1_ref, f32[8,768]{1,0:T(8,128)} %get-tuple-element.67.small2_ref, f32[4,1,640]{2,1,0:T(1,128)} %get-tuple-element.68.gbias_att_ref, ...), custom_call_target="tpu_custom_call" | custom-call | tf_op jit(solution)/shard_map/reduce_attention/pallas_call | solution.py:968
  267.5 2.3 unpack.1
  269.8 0.0 copy-done
  269.8 1.0 copy.40
Async XLA Ops:
  213.0 56.8 %copy-start = (bf16[784,768]{1,0:T(8,128)(2,1)S(1)}, bf16[784,768]{1,0:T(8,128)(2,1)}, u32[]{:S(2)}) copy-start(bf16[784,768]{1,0:T(8,128)(2,1)} %get-tuple-element.112) | copy-start | bytes 3612676

commit v4 on v3

--- a/solution.py
+++ b/solution.py
@@ -16,7 +16,9 @@
 VMEM_LIMIT = 60 * 1024 * 1024
 MLP_BEGIN = 11
 MLP_SLOTS = tuple(range(3, 48, 3))
-SUM_SLOTS = (3, 3, 6, 6, 9, 12, 15, 15, 18, 18, 21, 21, 24, 24, 27, 27, 30, 33, 36)
+SUM_SLOTS = (3, 3, 6, 6, 12, 15, 18, 21, 21, 24, 24, 27, 27, 30, 30, 33, 36, 39, 39)
+
+FOLDS = (3, 6, 9, 12, 15)
 
 
 def nn(left, right):
@@ -238,8 +240,8 @@
         near = [lambda k=k: self.from_near(k) for k in range(4)]
         line = [lambda k=k: self.from_line(k) for k in range(4)]
         self.steps = [
-            core[1, 1], core[1, 0], core[0, 1], core[0, 0], far[1][3], far[1][2], far[1][1], near[3], far[1][0], near[2],
-            far[0][3], near[1], far[0][2], line[3], near[0], far[0][1], line[2], far[0][0], line[1],
+            core[1, 1], core[1, 0], core[0, 1], core[0, 0], far[1][3], far[0][3], far[1][2], near[3], far[0][2], line[3],
+            far[1][1], near[2], far[0][1], line[2], far[1][0], near[1], far[0][0], line[1], near[0],
         ]
         self.last = line[0]
 
@@ -284,9 +286,10 @@
         self.core_copy(a, b).wait_recv()
         for z in range(4):
             self.held[a, b, z] = self.held[a, b, z] + self.core_in[a, b, z]
-        if a == 1:
+        if (a, b) == (1, 0):
             for k in (3, 2, 1, 0):
-                self.far_copy(b, self.at.near(k)).start()
+                for side in (1, 0):
+                    self.far_copy(side, self.at.near(k)).start()
 
     def from_far(self, b, k):
         z = self.at.near(k)
@@ -415,8 +418,8 @@
     exchange(0).start()
     for number, step in enumerate(scatter.steps):
         step()
-        if number in (1, 3, 4, 7, 10):
-            fold((1, 3, 4, 7, 10).index(number))
+        if number in FOLDS:
+            fold(FOLDS.index(number))
     scatter.finish()
     for index in range(5):
         exchange(index).wait_send()

time: 271 us -> 260 us (0.959)
  Pallas kernels: 262 us -> 251 us
    pallas_call x1, Pallas kernels: 54.5 us -> 47.1 us  [shards(): pl.pallas_call(reduce_kernel, in_specs=[any_spec] + [vmem_spec] * 5, out_...]
    pallas_call x1, Pallas kernels: 75.5 us -> 71.3 us  [shards(): pl.pallas_call(partial(attend_back_kernel, windows=windows, padded=padded...]
where the time goes in v4:
time: 260 us; the launch traced here: 259 us
  Pallas kernels  251 us (97%)
  local copies, waits for them, and re-layouts  3.94 us (2%)
  other arithmetic  3.86 us (1%)
    pallas_call x1, Pallas kernels, shards(): pl.pallas_call(partial(attend_kernel, windows=windows, padded=padded, key...  93 us
    pallas_call x1, Pallas kernels, shards(): pl.pallas_call(partial(attend_back_kernel, windows=windows, padded=padded...  71.3 us
    pallas_call x1, Pallas kernels, shards(): pl.pallas_call(reduce_kernel, in_specs=[any_spec] + [vmem_spec] * 5, out_...  47.1 us
    pallas_call x1, Pallas kernels, shards(): pl.pallas_call(partial(mlp_kernel, windows=windows, padded=padded), grid=...  37 us

profile of v4, /device:TPU:1, one launch (start us, length us, event | category | flops | bytes accessed | tf_op | source)
XLA Modules:
  0.0 259.2 jit_solution(14189273437128340436)
XLA Ops:
  0.7 1.2 pad_bitcast_fusion.refs_6_.slots_ref
  1.8 1.4 select_maximum_fusion.refs_5_
  3.2 0.9 copy.38
  4.1 0.9 slice_bitcast_fusion.2
  4.9 0.1 maximum_bitcast_fusion
  5.0 0.7 pad_maximum_fusion.1.refs_10_
  5.7 1.7 pad_maximum_fusion.refs_11_
  7.4 93.0 %attend.1 = (bf16[4,3,832,128]{3,2,1,0:T(8,128)(2,1)}, bf16[4,3,4,256,128]{4,3,2,1,0:T(8,128)(2,1)}, bf16[4,3,4,256,128]{4,3,2,1,0:T(8,128)(2,1)}, bf16[4,832,25...) custom-call(bf16[784,768]{1,0:T(8,128)(2,1)} %refs_0_.1, ...), custom_call_target="tpu_custom_call" | custom-call | tf_op jit(solution)/shard_map/attend/pallas_call | solution.py:860
  100.4 37.0 %mlp.1 = (bf16[784,768]{1,0:T(8,128)(2,1)}, f32[832,768]{1,0:T(8,128)}, bf16[8,4,2,96,768]{4,3,2,1,0:T(8,128)(2,1)}, f32[4,1,768]{2,1,0:T(1,128)}, f32[8,768]{1,0:T(8,128)}) custom-call(bf16[832,768]{1,0:T(8,128)(2,1)} %get-tuple-element.53.x_ref.refs_0_, f32[832,768]{1,0:T(8,128)} %get-tuple-element.54.attn_ref, bf16[784,768]{1,0:T(8,128)(2,1)} %cotangent_ref.1, ...), custom_call_target="tpu_custom_call" | custom-call | tf_op jit(solution)/shard_map/mlp/pallas_call | solution.py:899
  137.4 71.3 %attend_back.1 = (bf16[784,768]{1,0:T(8,128)(2,1)}, bf16[8,4,2,96,384]{4,3,2,1,0:T(8,128)(2,1)}, f32[8,768]{1,0:T(8,128)}, f32[4,1,640]{2,1,0:T(1,128)}, f32[128,128]{1,0:T(8,128)}, /*index=5*/f32[2,96,768]{2,1,0:T(8,128)}) custom-call(bf16[832,768]{1,0:T(8,128)(2,1)} %get-tuple-element.53.x_ref.refs_0_, f32[832,768]{1,0:T(8,128)} %get-tuple-element.57.refs_1_, ...), custom_call_target="tpu_custom_call" | custom-call | tf_op jit(solution)/shard_map/attend_back/pallas_call | solution.py:929
  208.7 0.0 copy-start
  208.7 47.1 %reduce_attention.1 = (f32[2,96,384]{2,1,0:T(8,128)}, f32[144,128]{1,0:T(8,128)}) custom-call(bf16[4,2,4,2,96,384]{5,4,3,2,1,0:T(8,128)(2,1)} %bitcast.22, f32[8,768]{1,0:T(8,128)} %get-tuple-element.66.small1_ref, f32[8,768]{1,0:T(8,128)} %get-tuple-element.67.small2_ref, f32[4,1,640]{2,1,0:T(1,128)} %get-tuple-element.68.gbias_att_ref, ...), custom_call_target="tpu_custom_call" | custom-call | tf_op jit(solution)/shard_map/reduce_attention/pallas_call | solution.py:971
  255.9 2.3 unpack.1
  258.2 0.0 copy-done
  258.2 1.0 copy.40
Async XLA Ops:
  208.7 49.4 %copy-start = (bf16[784,768]{1,0:T(8,128)(2,1)S(1)}, bf16[784,768]{1,0:T(8,128)(2,1)}, u32[]{:S(2)}) copy-start(bf16[784,768]{1,0:T(8,128)(2,1)} %get-tuple-element.112) | copy-start | bytes 3612676

commit v5 on v4

--- a/solution.py
+++ b/solution.py
@@ -15,8 +15,8 @@
 AXES = ("dp", "tensor")
 VMEM_LIMIT = 60 * 1024 * 1024
 MLP_BEGIN = 11
-MLP_SLOTS = tuple(range(3, 48, 3))
-SUM_SLOTS = (3, 3, 6, 6, 12, 15, 18, 21, 21, 24, 24, 27, 27, 30, 30, 33, 36, 39, 39)
+MLP_SLOTS = tuple(range(1, 16))
+SUM_SLOTS = (1, 1, 2, 2, 4, 5, 6, 7, 7, 8, 8, 9, 9, 10, 10, 11, 12, 13, 13)
 
 FOLDS = (3, 6, 9, 12, 15)
 
@@ -520,6 +520,9 @@
     pad_key = jnp.where(pad_lane == 79, NEGATIVE, 0.0).astype(BF)
 
     def window(w, carry):
+        for slot in duties:
+            for act in duties[slot]:
+                pl.when(step * windows + w == slot)(act)
         rows = pl.ds(pl.multiple_of(w * padded, 16), padded)
         qk = qk_ref[rows, :]
         vv = vv_ref[rows, :]
@@ -535,10 +538,6 @@
         ones = jnp.where((lane == 64) | (lane == 65), 1.0, 0.0)
         outs = []
         for head in range(3):
-            for slot in duties:
-                if slot % 3 == head:
-                    for act in duties[slot]:
-                        pl.when(step * windows + w == slot // 3)(act)
             moved = shift_lanes(spread[:, head * 128 : head * 128 + 128], amounts, True)
             high = moved.astype(BF).astype(F32)
             rest = pltpu.roll(moved - high, 16, 1)
@@ -575,7 +574,7 @@
         @pl.when(step == pl.num_programs(0) - 1)
         def _():
             for slot in duties:
-                if slot >= 48:
+                if slot >= 16:
                     for act in duties[slot]:
                         act()
             mlp.arrive()
@@ -682,6 +681,9 @@
     kept = (lane >= 64) & (field < 14)
 
     def window(w, carry):
+        if linked:
+            for slot, act in zip(SUM_SLOTS, scatter.steps):
+                pl.when(step * windows + w == slot)(act)
         rows = pl.ds(pl.multiple_of(w * padded, 16), padded)
         do = do_ref[rows, :].astype(F32)
         out = out_ref[0, rows, :].astype(F32)
@@ -694,10 +696,6 @@
         ]
         gq, gk, gv = [], [], []
         for head in range(3):
-            if linked:
-                for slot, act in zip(SUM_SLOTS, scatter.steps):
-                    if slot % 3 == head:
-                        pl.when(step * windows + w == slot // 3)(act)
             delta = -sums[head]
             first = delta.astype(BF).astype(F32)
             grad_out = jnp.where(low, grads[head], jnp.where(lane == 64, first, jnp.where(lane == 65, delta - first, 0.0))).astype(BF)
@@ -747,7 +745,7 @@
         small_ref[3:8, :] = jnp.zeros_like(small_ref[3:8, :])
         if linked:
             for slot, act in zip(SUM_SLOTS, scatter.steps):
-                if slot >= 48:
+                if slot >= 16:
                     act()
             scatter.finish()
 

time: 260 us -> 257 us (0.988)
  Pallas kernels: 251 us -> 247 us
where the time goes in v5:
time: 257 us; the launch traced here: 256 us
  Pallas kernels  247 us (96%)
  local copies, waits for them, and re-layouts  3.94 us (2%)
  other arithmetic  3.86 us (2%)
    pallas_call x1, Pallas kernels, shards(): pl.pallas_call(partial(attend_kernel, windows=windows, padded=padded, key...  91.4 us
    pallas_call x1, Pallas kernels, shards(): pl.pallas_call(partial(attend_back_kernel, windows=windows, padded=padded...  70.7 us
    pallas_call x1, Pallas kernels, shards(): pl.pallas_call(reduce_kernel, in_specs=[any_spec] + [vmem_spec] * 5, out_...  46 us
    pallas_call x1, Pallas kernels, shards(): pl.pallas_call(partial(mlp_kernel, windows=windows, padded=padded), grid=...  37 us

profile of v5, /device:TPU:1, one launch (start us, length us, event | category | flops | bytes accessed | tf_op | source)
XLA Modules:
  0.0 255.9 jit_solution(12405900370576341669)
XLA Ops:
  0.7 1.2 pad_bitcast_fusion.refs_6_.slots_ref
  1.8 1.4 select_maximum_fusion.refs_5_
  3.2 0.9 copy.38
  4.1 0.9 slice_bitcast_fusion.2
  4.9 0.1 maximum_bitcast_fusion
  5.0 0.7 pad_maximum_fusion.1.refs_10_
  5.7 1.7 pad_maximum_fusion.refs_11_
  7.4 91.4 %attend.1 = (bf16[4,3,832,128]{3,2,1,0:T(8,128)(2,1)}, bf16[4,3,4,256,128]{4,3,2,1,0:T(8,128)(2,1)}, bf16[4,3,4,256,128]{4,3,2,1,0:T(8,128)(2,1)}, bf16[4,832,25...) custom-call(bf16[784,768]{1,0:T(8,128)(2,1)} %refs_0_.1, ...), custom_call_target="tpu_custom_call" | custom-call | tf_op jit(solution)/shard_map/attend/pallas_call | solution.py:858
  98.9 37.0 %mlp.1 = (bf16[784,768]{1,0:T(8,128)(2,1)}, f32[832,768]{1,0:T(8,128)}, bf16[8,4,2,96,768]{4,3,2,1,0:T(8,128)(2,1)}, f32[4,1,768]{2,1,0:T(1,128)}, f32[8,768]{1,0:T(8,128)}) custom-call(bf16[832,768]{1,0:T(8,128)(2,1)} %get-tuple-element.53.x_ref.refs_0_, f32[832,768]{1,0:T(8,128)} %get-tuple-element.54.attn_ref, bf16[784,768]{1,0:T(8,128)(2,1)} %cotangent_ref.1, ...), custom_call_target="tpu_custom_call" | custom-call | tf_op jit(solution)/shard_map/mlp/pallas_call | solution.py:897
  135.9 70.7 %attend_back.1 = (bf16[784,768]{1,0:T(8,128)(2,1)}, bf16[8,4,2,96,384]{4,3,2,1,0:T(8,128)(2,1)}, f32[8,768]{1,0:T(8,128)}, f32[4,1,640]{2,1,0:T(1,128)}, f32[128,128]{1,0:T(8,128)}, /*index=5*/f32[2,96,768]{2,1,0:T(8,128)}) custom-call(bf16[832,768]{1,0:T(8,128)(2,1)} %get-tuple-element.53.x_ref.refs_0_, f32[832,768]{1,0:T(8,128)} %get-tuple-element.57.refs_1_, ...), custom_call_target="tpu_custom_call" | custom-call | tf_op jit(solution)/shard_map/attend_back/pallas_call | solution.py:927
  206.6 0.0 copy-start
  206.6 46.0 %reduce_attention.1 = (f32[2,96,384]{2,1,0:T(8,128)}, f32[144,128]{1,0:T(8,128)}) custom-call(bf16[4,2,4,2,96,384]{5,4,3,2,1,0:T(8,128)(2,1)} %bitcast.22, f32[8,768]{1,0:T(8,128)} %get-tuple-element.66.small1_ref, f32[8,768]{1,0:T(8,128)} %get-tuple-element.67.small2_ref, f32[4,1,640]{2,1,0:T(1,128)} %get-tuple-element.68.gbias_att_ref, ...), custom_call_target="tpu_custom_call" | custom-call | tf_op jit(solution)/shard_map/reduce_attention/pallas_call | solution.py:969
  252.6 2.3 unpack.1
  254.9 0.0 copy-done
  254.9 1.0 copy.40
Async XLA Ops:
  206.6 48.3 %copy-start = (bf16[784,768]{1,0:T(8,128)(2,1)S(1)}, bf16[784,768]{1,0:T(8,128)(2,1)}, u32[]{:S(2)}) copy-start(bf16[784,768]{1,0:T(8,128)(2,1)} %get-tuple-element.112) | copy-start | bytes 3612676
